TPU v7x, 32 devices: a whole 2x2x4 slice. The times are simulated.
32 devices in a mesh: dom: 8 (over y, x, core), cls: 4 (over z).
Axes of the slice: x: 2, y: 2, z: 4, core: 2. Of those that a mesh axis runs over, the one named last changes fastest.
Arguments:
- particles: bfloat16 [4096, 9216], P(('dom', 'cls')), may hold values from -6 to 6
- references: bfloat16 [200, 9216], P('cls', 'dom'), may hold values from -0.0625 to 0.0625
- owner: int32 [4096, 1], P(('dom', 'cls')), may hold values from 0 to 3; in each aligned block of 128 rows (0 to 127, 128 to 255, ...) at most 64 rows name the same one
- class_offset: int32 [4096], P(('dom', 'cls')), may hold values from 0 to 49
- rotation: int32 [4096], P(('dom', 'cls')), may hold values from 0 to 71
- shifts: int32 [4096, 2], P(('dom', 'cls')), may hold values from -6 to 6
- ctf_group: int32 [4096], P(('dom', 'cls')), may hold values from 0 to 63, as said below
- ctf_table: float32 [64, 64], replicated, may hold values from -6 to 6
Outputs:
- best_score: float32 [4096], P(('dom', 'cls'))
- new_references: float32 [200, 9216], P('cls', 'dom')
Inputs may be any that keep to these rules, and one draw needn't show every extreme that they name: Among the particles of one device no owner index is named more than 64 times, a bound that some block reaches. `ctf_group`: the particles of device block i (rows i * 128 to (i + 1) * 128 - 1) use only groups i * 2 to (i + 1) * 2 - 1.
All inputs are finite; a program needn't handle non-finite values.
Results may differ from a plain program's by a relative error of at most 0.0029.
Values may be sent and summed in bfloat16 or wider, within the bound.
A program may use at most 128 MiB of HBM per device.

v0:
```python
import math

import jax
import jax.numpy as jnp
from jax import lax
from jax.experimental import pallas as pl
from jax.experimental.pallas import tpu as pltpu
from jax.sharding import PartitionSpec as P

BOX = 128
tau_reg = 1.0
ROWS = 16
F32 = jnp.float32
BF16 = jnp.bfloat16
MESH = pl.DeviceIdType.MESH


def split_angles(angles):
    even = angles & -angles
    return even, angles // even


def lin(terms):
    total = None
    for factor, value in terms:
        if value is None or abs(factor) < 1e-12:
            continue
        if total is None:
            total = value if abs(factor - 1) < 1e-12 else (-value if abs(factor + 1) < 1e-12 else value * factor)
        elif abs(factor - 1) < 1e-12:
            total = total + value
        elif abs(factor + 1) < 1e-12:
            total = total - value
        else:
            total = total + value * factor
    return total


def add(a, b):
    return b if a is None else (a if b is None else a + b)


def sub(a, b):
    if b is None:
        return a
    return -b if a is None else a - b


def turn(re, im, part, whole):
    if part == 0:
        return re, im
    c, s = math.cos(2 * math.pi * part / whole), math.sin(2 * math.pi * part / whole)
    return lin([(c, re), (-s, im)]), lin([(s, re), (c, im)])


def odd_dft(values, sign, wanted):
    n = len(values)
    half = n // 2
    sums = [(add(values[j][0], values[n - j][0]), add(values[j][1], values[n - j][1])) for j in range(1, half + 1)]
    diffs = [(sub(values[j][0], values[n - j][0]), sub(values[j][1], values[n - j][1])) for j in range(1, half + 1)]
    out = {}
    for k in range(half + 1):
        pair = [x for x in (k, n - k) if x in wanted]
        if not pair:
            continue
        cs = [math.cos(2 * math.pi * ((j * k) % n) / n) for j in range(1, half + 1)]
        sn = [sign * math.sin(2 * math.pi * ((j * k) % n) / n) for j in range(1, half + 1)]
        even_re = lin([(1.0, values[0][0])] + [(c, s[0]) for c, s in zip(cs, sums)])
        even_im = lin([(1.0, values[0][1])] + [(c, s[1]) for c, s in zip(cs, sums)])
        odd_re = lin([(-s, d[1]) for s, d in zip(sn, diffs)])
        odd_im = lin([(s, d[0]) for s, d in zip(sn, diffs)])
        for x in pair:
            if x == k:
                out[x] = (add(even_re, odd_re), add(even_im, odd_im))
            else:
                out[x] = (sub(even_re, odd_re), sub(even_im, odd_im))
    return out


def real_even_dft(values):
    n = len(values)
    half = n // 2
    sums = [add(values[j], values[n - j]) for j in range(1, half)]
    diffs = [sub(values[j], values[n - j]) for j in range(1, half)]
    plus, minus = values[0] + values[half], values[0] - values[half]
    out = []
    for k in range(half + 1):
        cs = [math.cos(2 * math.pi * j * k / n) for j in range(1, half)]
        sn = [math.sin(2 * math.pi * j * k / n) for j in range(1, half)]
        re = lin([(1.0, minus if k % 2 else plus)] + list(zip(cs, sums)))
        im = lin([(-s, d) for s, d in zip(sn, diffs)]) if 0 < k < half else None
        out.append((re, im))
    return out


def forward_fft(load, store, angles):
    n1, n2 = split_angles(angles)
    inner = [real_even_dft([load(n2 * i + j) for i in range(n1)]) for j in range(n2)]
    for k1 in range(n1 // 2 + 1):
        values = [turn(*inner[j][k1], -((j * k1) % angles), angles) for j in range(n2)]
        for k2 in range(n2):
            pass
        wanted = set(range(n2)) if 0 < k1 < n1 // 2 else set(range(n2 // 2 + 1))
        for k2, (re, im) in odd_dft(values, -1.0, wanted).items():
            m = k1 + n1 * k2
            if m > angles // 2:
                m, im = angles - m, (None if im is None else -im)
            store(m, re, im)


def inverse_max(load, angles):
    n1, n2 = split_angles(angles)

    def value(m):
        if m == 0 or m == angles // 2:
            return load(m, 0), None
        if m > angles // 2:
            re, im = load(angles - m, 0), load(angles - m, 1)
            return re, -im
        return load(m, 0), load(m, 1)

    grid = []
    for k1 in range(n1 // 2 + 1):
        values = [value((k1 + n1 * k2) % angles) for k2 in range(n2)]
        got = odd_dft(values, 1.0, set(range(n2)))
        row = []
        for j in range(n2):
            row.append(turn(*got[j], (j * k1) % angles, angles))
        grid.append(row)
    best = None
    half = n1 // 2
    for j in range(n2):
        h0, h4 = grid[0][j][0], grid[half][j][0]
        plus, minus = h0 + h4, h0 - h4
        doubled = [(2.0 * grid[k][j][0], 2.0 * grid[k][j][1]) for k in range(1, half)]
        for i in range(half + 1):
            even = lin([(1.0, minus if i % 2 else plus)] + [(math.cos(2 * math.pi * i * (k + 1) / n1), doubled[k][0]) for k in range(half - 1)])
            odd = lin([(-math.sin(2 * math.pi * i * (k + 1) / n1), doubled[k][1]) for k in range(half - 1)]) if 0 < i < half else None
            top = even if odd is None else even + jnp.abs(odd)
            best = top if best is None else jnp.maximum(best, top)
    return best


def sin_cos_turns(u):
    u = u - jnp.floor(u + 0.5)
    v = (u * u) * (4 * math.pi * math.pi)
    s = jnp.full_like(v, 1.0 / math.factorial(17))
    for k in (15, 13, 11, 9, 7, 5, 3, 1):
        s = s * v + ((-1.0) ** (k // 2)) / math.factorial(k)
    c = jnp.full_like(v, -1.0 / math.factorial(18))
    for k in (16, 14, 12, 10, 8, 6, 4, 2, 0):
        c = c * v + ((-1.0) ** (k // 2)) / math.factorial(k)
    return s * (u * (2 * math.pi)), c


def fused(dims, part_hbm, refs_ref, shift_ref, turn_ref, owner_ref, offset_ref, group_ref, table_ref,
          best_ref, new_ref,
          part_ref, ux_ref, uy_ref, ctf_ref, rot_ref, meta_ref, buf, wch, ych, spec_p, spec_r, cross, contrib, got, metas, part, wpart, sbuf, rbuf, wrecv, sel_ref, mid, mgot, jsend, jrecv,
          part_sem, own_sem, zsend, zrecv, psend, precv, csend, crecv, asend, arecv, msend, mrecv,
          ssend, srecv, wsend, wrecv_sem):
    D, Z, angles, cyc = dims
    dom, zed = lax.axis_index("dom"), lax.axis_index("cls")
    rows, lanes = part_ref.shape[0], 2 * cyc
    local, width = refs_ref.shape
    pad = part.shape[1]
    bits = [1 << i for i in range(1, D.bit_length() - 1)]
    offsets = list(range(0, D, 2))

    def to_dom(q):
        return {"dom": dom ^ q, "cls": zed}

    def to_cls(j):
        return {"dom": dom, "cls": lax.rem(zed + j, Z)}

    def behind(j):
        return lax.rem(zed + (Z - j), Z)

    def remote(src, dst, s, r, where):
        return pltpu.make_async_remote_copy(src_ref=src, dst_ref=dst, send_sem=s, recv_sem=r,
                                            device_id=where, device_id_type=MESH)

    def block(q, j):
        return buf.at[dom ^ q, behind(j)]

    def z_copy(j):
        return remote(refs_ref, buf.at[dom, zed], zsend.at[j], zrecv.at[j], to_cls(j))

    def plane_copy(child, bit, j):
        q = child ^ bit
        src = refs_ref if q == 0 and j == 0 else block(q, j)
        return remote(src, block(q, j), psend.at[child // 2, j], precv.at[child // 2, j], to_dom(bit))

    def core_copy(q, j):
        src = refs_ref if q == 0 and j == 0 else block(q, j)
        return remote(src, block(q, j), csend.at[q // 2, j], crecv.at[q // 2, j], to_dom(1))

    def last_bit(q, j):
        return (1 << (q.bit_length() - 1)) if j % 2 == 0 else (q & -q)

    fetch = pltpu.make_async_copy(part_hbm, part_ref, part_sem)
    fetch.start()
    barrier = pltpu.get_barrier_semaphore()
    for q in range(1, D):
        pl.semaphore_signal(barrier, inc=1, device_id=to_dom(q), device_id_type=MESH)
    for j in range(1, Z):
        pl.semaphore_signal(barrier, inc=1, device_id=to_cls(j), device_id_type=MESH)
    meta_ref[...] = jnp.zeros_like(meta_ref)
    meta_ref[pl.ds(0, 1), :] = owner_ref[...] * pad + offset_ref[...]
    meta_ref[pl.ds(1, 1), :] = group_ref[...]
    pl.semaphore_wait(barrier, D + Z - 2)

    own = pltpu.make_async_copy(refs_ref, buf.at[dom, zed], own_sem)
    own.start()
    for j in range(1, Z):
        z_copy(j).start()

    def children(q, j):
        return [(q ^ b, b) for b in bits if not q & b and last_bit(q ^ b, j) == b]

    def event(q, j):
        if q:
            plane_copy(q, last_bit(q, j), j).wait_recv()
        elif j:
            z_copy(j).wait_recv()
        for child, b in children(q, j):
            plane_copy(child, b, j).start()
        core_copy(q, j).start()

    event(0, 0)
    for q in range(1, D):
        remote(meta_ref, metas.at[q], msend.at[q], mrecv.at[q], to_dom(q)).start()
    metas[0] = meta_ref[...]

    def column(row):
        return jnp.transpose(jnp.broadcast_to(row.astype(F32), (lanes, rows)))

    radius = (lax.rem(lax.broadcasted_iota(jnp.int32, (rows, lanes), 1), cyc) + 1).astype(F32) / BOX
    ux_ref[...] = column(shift_ref[pl.ds(0, 1), :]) * radius
    uy_ref[...] = column(shift_ref[pl.ds(1, 1), :]) * radius
    rot_ref[...] = column(turn_ref[...]).astype(jnp.int32)
    groups = table_ref.shape[0]
    table = table_ref[...]
    gcol = column(group_ref[...]).astype(jnp.int32)
    gcol = jnp.concatenate([gcol] * -(-groups // lanes), axis=1)[:, :groups]
    pick = jnp.where(gcol == lax.broadcasted_iota(jnp.int32, (rows, groups), 1), 1.0, 0.0)
    one = jnp.dot(pick, table, precision=lax.Precision.HIGHEST, preferred_element_type=F32)
    ctf_ref[...] = jnp.concatenate([one, one], axis=1)

    rank = {(q, j): bin(q).count("1") for j in range(Z) for q in offsets if q or j}
    events = sorted(rank, key=lambda e: (rank[e], e[1], e[0]))
    fetch.wait()
    chunks = rows // ROWS
    left = lax.broadcasted_iota(jnp.int32, (ROWS, lanes), 1) < cyc
    low, high = split_angles(angles)

    def piece(ref, sl, a):
        if width % lanes == 0:
            return ref(a * lanes // width)[sl, pl.ds(a * lanes % width, lanes)]
        halves = [(a * lanes + h * cyc) for h in range(2)]
        return jnp.concatenate([ref(c // width)[sl, pl.ds(c % width, cyc)] for c in halves], axis=1)

    def prep_chunk(i, carry):
        sl = pl.ds(pl.multiple_of(i * ROWS, ROWS), ROWS)
        ux, uy, ctf = ux_ref[sl, :], uy_ref[sl, :], ctf_ref[sl, :]
        for a in range(angles // 2):
            th = 2 * math.pi * a / angles
            s, c = sin_cos_turns(ux * math.cos(th) + uy * math.sin(th))
            s = jnp.where(left, -s, s) * ctf
            c = c * ctf
            for b, sign in ((a, 1), (a + angles // 2, -1)):
                x = part_ref[sl, pl.ds(b * lanes, lanes)].astype(F32)
                y = pltpu.roll(x, cyc, 1) * s
                w = x * c + y if sign > 0 else x * c - y
                wch[b] = w.astype(BF16).astype(F32)

        def store(m, re, im):
            first = re.astype(BF16)
            second = jnp.zeros_like(first) if im is None else im.astype(BF16)
            lower = pl.ds(pl.multiple_of(rows + i * ROWS, ROWS), ROWS)
            spec_p[m, sl, pl.ds(0, lanes)] = first
            spec_p[m, sl, pl.ds(lanes, lanes)] = second
            spec_p[m, lower, pl.ds(0, lanes)] = second
            spec_p[m, lower, pl.ds(lanes, lanes)] = -first

        forward_fft(lambda a: wch[a], store, angles)
        rot = rot_ref[sl, :]
        memo = {}

        def staged(level, a):
            a = a % angles
            if (level, a) not in memo:
                if level == 0:
                    memo[level, a] = wch[a]
                else:
                    step = 1 << (level - 1)
                    on = (rot & step) != 0
                    memo[level, a] = jnp.where(on, staged(level - 1, a + step), staged(level - 1, a))
            return memo[level, a]

        levels = low.bit_length() - 1
        for a in range(angles):
            ych[a] = staged(levels, a)
        for r in range(low):
            line = [ych[r + low * j] for j in range(high)]
            for bit in range((high - 1).bit_length()):
                on = (rot & (low << bit)) != 0
                line = [jnp.where(on, line[(j + (1 << bit)) % high], line[j]) for j in range(high)]
            for j in range(high):
                a = r + low * j
                value = line[j].astype(BF16)
                if width % lanes == 0:
                    contrib[a * lanes // width, sl, pl.ds(a * lanes % width, lanes)] = value
                else:
                    for h in range(2):
                        col = a * lanes + h * cyc
                        contrib[col // width, sl, pl.ds(col % width, cyc)] = value[:, h * cyc:(h + 1) * cyc]
        for c in range(chunks):
            mine = events[len(events) * c // chunks:len(events) * (c + 1) // chunks]

            @pl.when(i == c)
            def _():
                for q, j in mine:
                    event(q, j)
        return carry

    lax.fori_loop(0, chunks, prep_chunk, 0)

    spans = [(0, width)]
    if width % lanes == 0 and width // lanes >= 3:
        n = width // lanes
        cuts = [0, n - n // 3 - max(1, n * 2 // 9), n - max(1, n * 2 // 9), n]
        spans = [(x * lanes, (y - x) * lanes) for x, y in zip(cuts[:-1], cuts[1:])]

    def contrib_copy(q, c):
        cols = pl.ds(*spans[c])
        return remote(contrib.at[dom ^ q, :, cols], got.at[q, :, cols], asend.at[q, c], arecv.at[q, c], to_dom(q))

    paired = len(bits) == 2
    parity = lax.rem(dom, 2)
    last, first = 2 + 2 * parity, 4 - 2 * parity

    def pair_copy(k, kind, c):
        cols = pl.ds(*spans[c])
        if k == 0:
            to, slot = dom ^ 1, 1
        else:
            goal = k - 1
            to = ((dom // 2) ^ (2 - goal)) * 2 + goal
            slot = 3 - jnp.where(parity == goal, 1, 0)
        chunk = to if kind == 0 else to ^ (2 + 2 * lax.rem(to, 2))
        return remote(contrib.at[chunk, :, cols], got.at[slot + 4 * kind, :, cols], asend.at[2 * k + kind, c],
                      arecv.at[slot + 4 * kind, c], {"dom": to, "cls": zed})

    def arrived(slot, kind, c):
        cols = pl.ds(*spans[c])
        return remote(contrib.at[0, :, cols], got.at[slot + 4 * kind, :, cols], asend.at[0, c],
                      arecv.at[slot + 4 * kind, c], to_dom(1))

    def joined(c):
        cols = pl.ds(*spans[c])
        return remote(mid.at[:, :, cols], mgot.at[:, :, cols], jsend.at[c], jrecv.at[c], {"dom": dom ^ last, "cls": zed})

    if paired:
        for kind, c in [(1, c) for c in range(len(spans))] + [(0, c) for c in range(len(spans))]:
            for k in range(3):
                pair_copy(k, kind, c).start()
        got[0] = contrib[dom]
        got[4] = contrib[dom ^ last]
    else:
        for c in range(len(spans)):
            for q in range(1, D):
                contrib_copy(q, c).start()
        got[0] = contrib[dom]

    for q in range(1, D):
        remote(meta_ref, metas.at[q], msend.at[q], mrecv.at[q], to_dom(q)).wait()
    ids = lax.broadcasted_iota(jnp.int32, (Z * pad, rows), 0)
    gids = lax.broadcasted_iota(jnp.int32, (groups, rows), 0)
    sel_ref[...] = jnp.concatenate([jnp.where(ids == metas[d, pl.ds(0, 1), :], 1.0, 0.0).astype(BF16) for d in range(D)], axis=1)
    gsel = jnp.concatenate([jnp.where(gids == metas[d, pl.ds(1, 1), :], 1.0, 0.0).astype(BF16) for d in range(D)], axis=1)
    counts = lax.dot_general(sel_ref[...], gsel, (((1,), (1,)), ((), ())), preferred_element_type=F32)
    wsum = jnp.dot(counts, table * table, precision=lax.Precision.HIGHEST, preferred_element_type=F32)
    wpart[...] = wsum.reshape(Z, pad, wsum.shape[1])

    def w_copy(j):
        return remote(wpart.at[lax.rem(zed + j, Z)], wrecv.at[j], wsend.at[j], wrecv_sem.at[j], to_cls(j))

    for j in range(1, Z):
        w_copy(j).start()

    def s_copy(j, c):
        cols = pl.ds(*spans[c])
        return remote(sbuf.at[lax.rem(zed + j, Z), :, cols], rbuf.at[j, :, cols], ssend.at[j, c], srecv.at[j, c], to_cls(j))

    def send_span(c):
        start, size = spans[c]
        cols = pl.ds(start, size)
        if paired:
            for slot in (1, 2, 3):
                arrived(slot, 0, c).wait_recv()
            sums = jnp.dot(sel_ref[:, pl.ds(0, 4 * rows)], got[0:4, :, cols].reshape(4 * rows, size), preferred_element_type=F32)
            sums = sums.reshape(Z, pad, size)
            joined(c).wait_recv()
            part[:, pl.ds(0, local), cols] = sums[:, :local, :] + mgot[:, :, cols].astype(F32)
        else:
            for q in range(1, D):
                contrib_copy(q, c).wait()
            sums = jnp.dot(sel_ref[...], got[:, :, cols].reshape(D * rows, size), preferred_element_type=F32)
            part[:, :, cols] = sums.reshape(Z, pad, size)
        sbuf[:, :, cols] = part[:, pl.ds(0, local), cols].astype(BF16)
        for j in range(1, Z):
            s_copy(j, c).start()

    own.wait()
    for j in range(Z):
        for q in offsets:
            core_copy(q, j).wait_recv()

    def ref_rows(z, start, count):
        sl = pl.ds(start, count)
        out = pl.ds(start, count)

        def store(m, re, im):
            second = jnp.zeros_like(re) if im is None else im
            spec_r[m, z, out, pl.ds(0, lanes)] = re.astype(BF16)
            spec_r[m, z, out, pl.ds(lanes, lanes)] = second.astype(BF16)

        forward_fft(lambda a: piece(lambda d: buf.at[d, z], sl, a).astype(F32), store, angles)

    whole = local // ROWS
    rest = local % ROWS

    def ref_step(n, carry):
        ref_rows(n // whole, pl.multiple_of((n % whole) * ROWS, ROWS), ROWS)
        return carry

    lax.fori_loop(0, Z * whole, ref_step, 0)
    if rest:
        def ref_rest(z, carry):
            ref_rows(z, whole * ROWS, rest)
            return carry
        lax.fori_loop(0, Z, ref_rest, 0)

    if paired:
        near = [metas[0, pl.ds(0, 1), :], metas[1, pl.ds(0, 1), :], metas[first, pl.ds(0, 1), :], metas[first ^ 1, pl.ds(0, 1), :]]
        sel4 = jnp.concatenate([jnp.where(ids == row, 1.0, 0.0).astype(BF16) for row in near], axis=1)
        sel_ref[:, pl.ds(0, 4 * rows)] = sel4
        for c, (start, size) in enumerate(spans):
            cols = pl.ds(start, size)
            for slot in (1, 2, 3):
                arrived(slot, 1, c).wait_recv()
            sums = jnp.dot(sel4, got[4:8, :, cols].reshape(4 * rows, size), preferred_element_type=F32)
            mid[:, :, cols] = sums.reshape(Z, pad, size)[:, :local, :].astype(BF16)
            joined(c).start()

    freqs = angles // 2 + 1

    def cross_step(m, carry):
        lhs = spec_r[m].reshape(Z * pad, 2 * lanes)
        cross[m] = lax.dot_general(lhs, spec_p[m], (((1,), (1,)), ((), ())), preferred_element_type=F32)
        return carry

    lax.fori_loop(0, freqs, cross_step, 0)
    if paired:
        for c in range(len(spans[:2])):
            send_span(c)
    groups_of = -(-local // 8)

    def back_step(n, best):
        z, j = n // groups_of, n % groups_of
        start = pl.multiple_of(z * pad + j * 8, 8)

        def load(m, p):
            return cross[m, pl.ds(start, 8), pl.ds(p * rows, rows)]

        top = inverse_max(load, angles)
        row = lax.broadcasted_iota(jnp.int32, (8, rows), 0) + j * 8
        return jnp.maximum(best, jnp.where(row < local, top, -jnp.inf))

    best = lax.fori_loop(0, Z * groups_of, back_step, jnp.full((8, rows), -jnp.inf, F32))
    best_ref[...] = jnp.max(best, axis=0, keepdims=True) * (1.0 / angles)

    for c in range(len(spans[:2]) if paired else 0, len(spans)):
        send_span(c)
    weight = wpart[zed][:local, :]
    for j in range(1, Z):
        w_copy(j).wait()
        weight = weight + wrecv[j][:local, :]
    scale = 1.0 / (jnp.concatenate([weight, weight], axis=1) + tau_reg)
    for c, (start, size) in enumerate(spans):
        cols = pl.ds(start, size)
        total = part[zed, :, cols][:local, :]
        for j in range(1, Z):
            s_copy(j, c).wait()
            total = total + rbuf[j, :, cols].astype(F32)
        new_ref[:, cols] = total * jnp.concatenate([scale] * -(-size // lanes), axis=1)[:, :size]

    if paired:
        for c in range(len(spans)):
            joined(c).wait_send()
            for k in range(3):
                for kind in range(2):
                    pair_copy(k, kind, c).wait_send()
    for j in range(1, Z):
        z_copy(j).wait_send()
    for j in range(Z):
        for q in offsets:
            core_copy(q, j).wait_send()
            if q:
                plane_copy(q, last_bit(q, j), j).wait_send()


def per_device(particles, references, owner, class_offset, rotation, shifts, ctf_group, ctf_table):
    D, Z = lax.axis_size("dom"), lax.axis_size("cls")
    groups, cyc = ctf_table.shape
    rows, full = particles.shape
    lanes = 2 * cyc
    angles = full // lanes
    local, width = references.shape
    pad = -(-local // ROWS) * ROWS
    freqs = angles // 2 + 1
    chunks = 3
    dma = pltpu.SemaphoreType.DMA
    best, new = pl.pallas_call(
        lambda *refs: fused((D, Z, angles, cyc), *refs),
        out_shape=(jax.ShapeDtypeStruct((1, rows), F32), jax.ShapeDtypeStruct((local, width), F32)),
        in_specs=[pl.BlockSpec(memory_space=pl.ANY)] * 2 + [pl.BlockSpec(memory_space=pltpu.VMEM)] * 6,
        out_specs=[pl.BlockSpec(memory_space=pltpu.VMEM)] * 2,
        scratch_shapes=[
            pltpu.VMEM((rows, full), BF16),
            pltpu.VMEM((rows, lanes), F32),
            pltpu.VMEM((rows, lanes), F32),
            pltpu.VMEM((rows, lanes), F32),
            pltpu.VMEM((rows, lanes), jnp.int32),
            pltpu.VMEM((8, rows), jnp.int32),
            pltpu.VMEM((D, Z, local, width), BF16),
            pltpu.VMEM((angles, ROWS, lanes), F32),
            pltpu.VMEM((angles, ROWS, lanes), F32),
            pltpu.VMEM((freqs, 2 * rows, 2 * lanes), BF16),
            pltpu.VMEM((freqs, Z, pad, 2 * lanes), BF16),
            pltpu.VMEM((freqs, Z * pad, 2 * rows), F32),
            pltpu.VMEM((D, rows, width), BF16),
            pltpu.VMEM((D, rows, width), BF16),
            pltpu.VMEM((D, 8, rows), jnp.int32),
            pltpu.VMEM((Z, pad, width), F32),
            pltpu.VMEM((Z, pad, cyc), F32),
            pltpu.VMEM((Z, local, width), BF16),
            pltpu.VMEM((Z, local, width), BF16),
            pltpu.VMEM((Z, pad, cyc), F32),
            pltpu.VMEM((Z * pad, D * rows), BF16),
            pltpu.VMEM((Z, local, width), BF16),
            pltpu.VMEM((Z, local, width), BF16),
            dma((chunks,)), dma((chunks,)),
            dma, dma, dma((Z,)), dma((Z,)),
            dma((D // 2, Z)), dma((D // 2, Z)), dma((D // 2, Z)), dma((D // 2, Z)),
            dma((D, chunks)), dma((D, chunks)), dma((D,)), dma((D,)),
            dma((Z, chunks)), dma((Z, chunks)), dma((Z,)), dma((Z,)),
        ],
        compiler_params=pltpu.CompilerParams(collective_id=0, has_side_effects=True,
                                             vmem_limit_bytes=60 << 20),
        name="class_pass",
    )(particles, references, shifts.T, rotation[None], owner.T, class_offset[None], ctf_group[None], ctf_table)
    return best[0], new


def solution(mesh):
    return jax.shard_map(
        per_device,
        mesh=mesh,
        in_specs=(
            P(("dom", "cls"), None),
            P("cls", "dom"),
            P(("dom", "cls"), None),
            P(("dom", "cls")),
            P(("dom", "cls")),
            P(("dom", "cls"), None),
            P(("dom", "cls")),
            P(),
        ),
        out_specs=(P(("dom", "cls")), P("cls", "dom")),
        check_vma=False,
    )
```

profile of v0, /device:TPU:0, one launch (start us, length us, event | category | flops | bytes accessed | tf_op | source)
XLA Modules:
  0.0 65.9 jit_solution(6980889332760298576)
XLA Ops:
  0.6 62.5 %class_pass.1 = (f32[1,128]{1,0:T(1,128)}, f32[50,1152]{1,0:T(8,128)}) custom-call(bf16[128,9216]{1,0:T(8,128)(2,1)} %refs_0_.1, bf16[50,1152]{1,0:T(8,128)(2,1)} %refs_1_.1, s32[2,128]{1,0:T(2,128)} %bitcast.6, s32[1,128]{1,0:T(1,128)} %bitcast.7, s32[1,128]{1,0:T(1,128)} %bitcast.8, s32[1,128]{1,0:T(1,128)} %bitcast.9, s32[1,128]{1,0:T(1,128)} %bitcast.10, ...), custom_call_target="tpu_custom_call" | custom-call | tf_op jit(solution)/shard_map/class_pass/pallas_call | solution.py:524
  63.1 1.1 %copy.12 = f32[128]{0:T(128)} copy(f32[128]{0:T(128)} %bitcast.11) | data formatting | bytes 1024
  64.2 1.7 %copy.13 = f32[50,1152]{1,0:T(8,128)} copy(f32[50,1152]{1,0:T(8,128)} %get-tuple-element.9) | data formatting | bytes 460800
where the time goes:
time: 66.6 us; the launch traced here: 65.9 us
  Pallas kernels  62.5 us (94%)
  local copies, waits for them, and re-layouts  2.79 us (4%)
    pallas_call x1, Pallas kernels, per_device(): pl.pallas_call(lambda *refs: fused((D, Z, angles, cyc), *refs), out_shape...  62.5 us
    unnamed x2, local copies, waits for them, and re-layouts  2.79 us

commit v1 on v0

--- a/solution.py
+++ b/solution.py
@@ -8,6 +8,8 @@
 from jax.sharding import PartitionSpec as P
 
 BOX = 128
+SPAN = 16
+EARLY = -0.5
 tau_reg = 1.0
 ROWS = 16
 F32 = jnp.float32
@@ -53,8 +55,33 @@
     return lin([(c, re), (-s, im)]), lin([(s, re), (c, im)])
 
 
+def three(a, b, c, sign):
+    tr, ti = add(b[0], c[0]), add(b[1], c[1])
+    er, ei = lin([(sign * math.sqrt(0.75), sub(b[0], c[0]))]), None
+    if b[1] is not None or c[1] is not None:
+        ei = lin([(sign * math.sqrt(0.75), sub(b[1], c[1]))])
+    mr = sub(a[0], lin([(0.5, tr)]))
+    mi = None if ti is None and a[1] is None else sub(a[1], lin([(0.5, ti)]))
+    first = (add(a[0], tr), None if a[1] is None and ti is None else add(a[1], ti))
+    second = (mr if ei is None else mr - ei, add(mi, er))
+    third = (mr if ei is None else mr + ei, -er if mi is None else mi - er)
+    return first, second, third
+
+
+def nine_dft(values, sign, wanted):
+    inner = [three(values[j], values[j + 3], values[j + 6], sign) for j in range(3)]
+    out = {}
+    for k in range(3):
+        row = [turn(*inner[j][k], sign * j * k, 9) for j in range(3)]
+        for l, x in enumerate(three(*row, sign)):
+            out[k + 3 * l] = x
+    return {k: out[k] for k in out if k in wanted}
+
+
 def odd_dft(values, sign, wanted):
     n = len(values)
+    if n == 9:
+        return nine_dft(values, sign, wanted)
     half = n // 2
     sums = [(add(values[j][0], values[n - j][0]), add(values[j][1], values[n - j][1])) for j in range(1, half + 1)]
     diffs = [(sub(values[j][0], values[n - j][0]), sub(values[j][1], values[n - j][1])) for j in range(1, half + 1)]
@@ -77,8 +104,19 @@
     return out
 
 
+def real_eight_dft(v):
+    r = math.sqrt(0.5)
+    s = [v[j] + v[j + 4] for j in range(4)]
+    d = [v[j] - v[j + 4] for j in range(4)]
+    a, b = s[0] + s[2], s[1] + s[3]
+    p, q = r * (d[1] - d[3]), r * (d[1] + d[3])
+    return [(a + b, None), (d[0] + p, -d[2] - q), (s[0] - s[2], s[3] - s[1]), (d[0] - p, d[2] - q), (a - b, None)]
+
+
 def real_even_dft(values):
     n = len(values)
+    if n == 8:
+        return real_eight_dft(values)
     half = n // 2
     sums = [add(values[j], values[n - j]) for j in range(1, half)]
     diffs = [sub(values[j], values[n - j]) for j in range(1, half)]
@@ -131,6 +169,17 @@
     half = n1 // 2
     for j in range(n2):
         h0, h4 = grid[0][j][0], grid[half][j][0]
+        if n1 == 8:
+            r = math.sqrt(2.0)
+            (a1, b1), (a2, b2), (a3, b3) = grid[1][j], grid[2][j], grid[3][j]
+            plus, minus = h0 + h4, h0 - h4
+            twice, sine = 2.0 * a2, 2.0 * b2
+            w, e = r * (a1 - a3), r * (b1 + b3)
+            tops = [plus + twice + 2.0 * jnp.abs(a1 + a3), plus - twice + 2.0 * jnp.abs(b1 - b3),
+                    minus + w + jnp.abs(e + sine), minus - w + jnp.abs(e - sine)]
+            for top in tops:
+                best = top if best is None else jnp.maximum(best, top)
+            continue
         plus, minus = h0 + h4, h0 - h4
         doubled = [(2.0 * grid[k][j][0], 2.0 * grid[k][j][1]) for k in range(1, half)]
         for i in range(half + 1):
@@ -155,9 +204,9 @@
 
 def fused(dims, part_hbm, refs_ref, shift_ref, turn_ref, owner_ref, offset_ref, group_ref, table_ref,
           best_ref, new_ref,
-          part_ref, ux_ref, uy_ref, ctf_ref, rot_ref, meta_ref, buf, wch, ych, spec_p, spec_r, cross, contrib, got, metas, part, wpart, sbuf, rbuf, wrecv, sel_ref, mid, mgot, jsend, jrecv,
+          part_ref, tab, phase, ctf_ref, rot_ref, meta_ref, buf, wch, ych, spec_p, spec_r, cross, contrib, got, metas, part, wpart, sbuf, rbuf, wrecv, sel_ref, keep, bsend, brecv, mid, mgot, jsend, jrecv,
           part_sem, own_sem, zsend, zrecv, psend, precv, csend, crecv, asend, arecv, msend, mrecv,
-          ssend, srecv, wsend, wrecv_sem):
+          ssend, srecv, wsend, wrecv_sem, xsend, xrecv):
     D, Z, angles, cyc = dims
     dom, zed = lax.axis_index("dom"), lax.axis_index("cls")
     rows, lanes = part_ref.shape[0], 2 * cyc
@@ -165,6 +214,10 @@
     pad = part.shape[1]
     bits = [1 << i for i in range(1, D.bit_length() - 1)]
     offsets = list(range(0, D, 2))
+    paired = len(bits) == 2
+    parity = lax.rem(dom, 2)
+    last, first = 2 + 2 * parity, 4 - 2 * parity
+    along = [0, D - 2] if paired else [0]
 
     def to_dom(q):
         return {"dom": dom ^ q, "cls": zed}
@@ -172,30 +225,53 @@
     def to_cls(j):
         return {"dom": dom, "cls": lax.rem(zed + j, Z)}
 
-    def behind(j):
-        return lax.rem(zed + (Z - j), Z)
+    near_first = [sorted(range(Z), key=lambda o: (abs(o - z), o)) for z in range(Z)]
+    origin = [sum(jnp.where(zed == z, near_first[z][k], 0) for z in range(Z)) for k in range(Z)]
 
     def remote(src, dst, s, r, where):
         return pltpu.make_async_remote_copy(src_ref=src, dst_ref=dst, send_sem=s, recv_sem=r,
                                             device_id=where, device_id_type=MESH)
 
-    def block(q, j):
-        return buf.at[dom ^ q, behind(j)]
-
-    def z_copy(j):
-        return remote(refs_ref, buf.at[dom, zed], zsend.at[j], zrecv.at[j], to_cls(j))
-
-    def plane_copy(child, bit, j):
+    def block(q, o):
+        return buf.at[dom ^ q, o]
+
+    def z_copy(src, q, o, up):
+        to = {"dom": dom, "cls": zed + 1 if up else zed - 1}
+        line = along.index(q)
+        return remote(src, buf.at[dom ^ q, o], zsend.at[1 if up else 0, line, o], zrecv.at[line, o], to)
+
+    def z_pass(src, q, o, moving_up, moving_down):
+        @pl.when(jnp.logical_and(moving_up, zed + 1 < Z))
+        def _():
+            z_copy(src, q, o, True).start()
+
+        @pl.when(jnp.logical_and(moving_down, zed > 0))
+        def _():
+            z_copy(src, q, o, False).start()
+
+    def source(q, o, h):
+        return refs_ref if q == 0 and h == 0 else block(q, o)
+
+    def plane_copy(child, bit, o, h):
         q = child ^ bit
-        src = refs_ref if q == 0 and j == 0 else block(q, j)
-        return remote(src, block(q, j), psend.at[child // 2, j], precv.at[child // 2, j], to_dom(bit))
-
-    def core_copy(q, j):
-        src = refs_ref if q == 0 and j == 0 else block(q, j)
-        return remote(src, block(q, j), csend.at[q // 2, j], crecv.at[q // 2, j], to_dom(1))
-
-    def last_bit(q, j):
-        return (1 << (q.bit_length() - 1)) if j % 2 == 0 else (q & -q)
+        return remote(source(q, o, h), block(q, o), psend.at[child // 2, o], precv.at[child // 2, o], to_dom(bit))
+
+    def core_copy(q, o, h):
+        return remote(source(q, o, h), block(q, o), csend.at[q // 2, o], crecv.at[q // 2, o], to_dom(1))
+
+    def last_bit(q, h):
+        return (1 << (q.bit_length() - 1)) if h % 2 == 0 else (q & -q)
+
+    def at_hops(h, act):
+        if h == 0:
+            act(zed, 0)
+            return
+        for side in (1, -1):
+            o = zed + side * h
+
+            @pl.when(jnp.logical_and(o >= 0, o < Z))
+            def _():
+                act(o, side)
 
     fetch = pltpu.make_async_copy(part_hbm, part_ref, part_sem)
     fetch.start()
@@ -207,36 +283,24 @@
     meta_ref[...] = jnp.zeros_like(meta_ref)
     meta_ref[pl.ds(0, 1), :] = owner_ref[...] * pad + offset_ref[...]
     meta_ref[pl.ds(1, 1), :] = group_ref[...]
-    pl.semaphore_wait(barrier, D + Z - 2)
-
-    own = pltpu.make_async_copy(refs_ref, buf.at[dom, zed], own_sem)
-    own.start()
-    for j in range(1, Z):
-        z_copy(j).start()
-
-    def children(q, j):
-        return [(q ^ b, b) for b in bits if not q & b and last_bit(q ^ b, j) == b]
-
-    def event(q, j):
-        if q:
-            plane_copy(q, last_bit(q, j), j).wait_recv()
-        elif j:
-            z_copy(j).wait_recv()
-        for child, b in children(q, j):
-            plane_copy(child, b, j).start()
-        core_copy(q, j).start()
-
-    event(0, 0)
-    for q in range(1, D):
-        remote(meta_ref, metas.at[q], msend.at[q], mrecv.at[q], to_dom(q)).start()
-    metas[0] = meta_ref[...]
-
     def column(row):
         return jnp.transpose(jnp.broadcast_to(row.astype(F32), (lanes, rows)))
 
-    radius = (lax.rem(lax.broadcasted_iota(jnp.int32, (rows, lanes), 1), cyc) + 1).astype(F32) / BOX
-    ux_ref[...] = column(shift_ref[pl.ds(0, 1), :]) * radius
-    uy_ref[...] = column(shift_ref[pl.ds(1, 1), :]) * radius
+    quarter, levels = angles // 4, tab.shape[1] // SPAN
+    left = lax.broadcasted_iota(jnp.int32, (SPAN, lanes), 1) < cyc
+    radius = (lax.rem(lax.broadcasted_iota(jnp.int32, (SPAN, lanes), 1), cyc) + 1).astype(F32) / BOX
+    radius = radius * (lax.broadcasted_iota(jnp.int32, (SPAN, lanes), 0) - SPAN // 2).astype(F32)
+    for a in range(quarter + 1):
+        s, c = sin_cos_turns(radius * (math.cos(2 * math.pi * a / angles) if a < quarter else 0.0))
+        for h, value in enumerate((c, jnp.where(left, -s, s))):
+            for n in range(levels):
+                tab[a, pl.ds(n * SPAN, SPAN), pl.ds(h * lanes, lanes)] = value.astype(BF16)
+                value = value - value.astype(BF16).astype(F32)
+    moved = jnp.concatenate([column(shift_ref[pl.ds(n, 1), :]) for n in range(2)], axis=0).astype(jnp.int32)
+    steps = lax.rem(lax.broadcasted_iota(jnp.int32, (2 * rows, levels * SPAN), 1), SPAN) - SPAN // 2
+    picked = jnp.where(moved[:, :levels * SPAN] == steps, 1.0, 0.0).astype(BF16)
+    for a in range(quarter + 1):
+        phase[a] = jnp.dot(picked, tab[a], preferred_element_type=F32)
     rot_ref[...] = column(turn_ref[...]).astype(jnp.int32)
     groups = table_ref.shape[0]
     table = table_ref[...]
@@ -246,11 +310,66 @@
     one = jnp.dot(pick, table, precision=lax.Precision.HIGHEST, preferred_element_type=F32)
     ctf_ref[...] = jnp.concatenate([one, one], axis=1)
 
-    rank = {(q, j): bin(q).count("1") for j in range(Z) for q in offsets if q or j}
-    events = sorted(rank, key=lambda e: (rank[e], e[1], e[0]))
+    pl.semaphore_wait(barrier, D + Z - 2)
+
+    own = pltpu.make_async_copy(refs_ref, buf.at[dom, zed], own_sem)
+    own.start()
+    z_pass(refs_ref, 0, zed, zed >= 0, zed >= 0)
+
+    def children(q, h):
+        return [(q ^ b, b) for b in bits if not q & b and last_bit(q ^ b, h) == b]
+
+    def event(q, h):
+        def act(o, side):
+            if h and q in along:
+                z_copy(refs_ref, q, o, True).wait_recv()
+                if side < 0:
+                    z_pass(block(q, o), q, o, zed >= 0, zed < 0)
+                else:
+                    z_pass(block(q, o), q, o, zed < 0, zed >= 0)
+            elif q:
+                plane_copy(q, last_bit(q, h), o, h).wait_recv()
+                if q in along:
+                    z_pass(block(q, o), q, o, zed >= 0, zed >= 0)
+            if not paired or q == 0:
+                for child, b in children(q, h):
+                    if not paired or child not in along:
+                        plane_copy(child, b, o, h).start()
+            elif h == 0 and q not in along:
+                @pl.when(first == D - 2 - q)
+                def _():
+                    plane_copy(D - 2, D - 2 - q, o, h).start()
+            core_copy(q, o, h).start()
+
+        at_hops(h, act)
+
+    event(0, 0)
+    for q in range(1, D):
+        remote(meta_ref, metas.at[q], msend.at[q], mrecv.at[q], to_dom(q)).start()
+    metas[0] = meta_ref[...]
+
+    plan = {}
+    for h in range(Z):
+        for q in sorted(offsets, key=lambda q: bin(q).count("1")):
+            hops = bin(q).count("1")
+            if not q and not h:
+                continue
+            if not paired:
+                spot = ("fft", h)
+            elif hops == 0:
+                spot = ("prep", 4) if h == 1 else ("prep", 7) if h == 2 else ("counted", 0) if h == 3 else ("fft", h - 1)
+            elif hops == 1:
+                spot = ("prep", 4) if h == 0 else ("summed", 0) if h == 1 else ("fft", h)
+            else:
+                spot = ("sent", 0) if h == 0 else ("fft", h)
+            plan.setdefault(spot, []).append((q, h))
+
+    def serve(*spot):
+        for q, h in plan.get(spot, []):
+            event(q, h)
+
     fetch.wait()
     chunks = rows // ROWS
-    left = lax.broadcasted_iota(jnp.int32, (ROWS, lanes), 1) < cyc
     low, high = split_angles(angles)
 
     def piece(ref, sl, a):
@@ -259,19 +378,30 @@
         halves = [(a * lanes + h * cyc) for h in range(2)]
         return jnp.concatenate([ref(c // width)[sl, pl.ds(c % width, cyc)] for c in halves], axis=1)
 
+    def twin_copy(i):
+        start = pl.multiple_of(i * ROWS, ROWS)
+        return remote(contrib.at[1, :, pl.ds(start, ROWS), :], contrib.at[0, :, pl.ds(rows + start, ROWS), :],
+                      xsend.at[i], xrecv.at[i], to_dom(1))
+
     def prep_chunk(i, carry):
         sl = pl.ds(pl.multiple_of(i * ROWS, ROWS), ROWS)
-        ux, uy, ctf = ux_ref[sl, :], uy_ref[sl, :], ctf_ref[sl, :]
-        for a in range(angles // 2):
-            th = 2 * math.pi * a / angles
-            s, c = sin_cos_turns(ux * math.cos(th) + uy * math.sin(th))
-            s = jnp.where(left, -s, s) * ctf
-            c = c * ctf
+        ctf = ctf_ref[sl, :]
+        also = pl.ds(pl.multiple_of(rows + i * ROWS, ROWS), ROWS)
+
+        def apply(a, c, s):
             for b, sign in ((a, 1), (a + angles // 2, -1)):
                 x = part_ref[sl, pl.ds(b * lanes, lanes)].astype(F32)
                 y = pltpu.roll(x, cyc, 1) * s
-                w = x * c + y if sign > 0 else x * c - y
-                wch[b] = w.astype(BF16).astype(F32)
+                wch[b] = (x * c + y if sign > 0 else x * c - y).astype(BF16)
+
+        for a in range(quarter + 1):
+            cx, sx = phase[a, sl, pl.ds(0, lanes)], phase[a, sl, pl.ds(lanes, lanes)]
+            cy = phase[quarter - a, also, pl.ds(0, lanes)] * ctf
+            sy = phase[quarter - a, also, pl.ds(lanes, lanes)] * ctf
+            cc, ss, sc, cs = cx * cy, sx * sy, sx * cy, cx * sy
+            apply(a, cc - ss, sc + cs)
+            if 0 < a < quarter:
+                apply(angles // 2 - a, cc + ss, cs - sc)
 
         def store(m, re, im):
             first = re.astype(BF16)
@@ -282,8 +412,9 @@
             spec_p[m, lower, pl.ds(0, lanes)] = second
             spec_p[m, lower, pl.ds(lanes, lanes)] = -first
 
-        forward_fft(lambda a: wch[a], store, angles)
+        forward_fft(lambda a: wch[a].astype(F32), store, angles)
         rot = rot_ref[sl, :]
+        bits_on = [jnp.where((rot & (1 << n)) != 0, 1.0, 0.0).astype(BF16) > 0 for n in range((angles - 1).bit_length())]
         memo = {}
 
         def staged(level, a):
@@ -293,7 +424,7 @@
                     memo[level, a] = wch[a]
                 else:
                     step = 1 << (level - 1)
-                    on = (rot & step) != 0
+                    on = bits_on[level - 1]
                     memo[level, a] = jnp.where(on, staged(level - 1, a + step), staged(level - 1, a))
             return memo[level, a]
 
@@ -303,24 +434,29 @@
         for r in range(low):
             line = [ych[r + low * j] for j in range(high)]
             for bit in range((high - 1).bit_length()):
-                on = (rot & (low << bit)) != 0
+                on = bits_on[levels + bit]
                 line = [jnp.where(on, line[(j + (1 << bit)) % high], line[j]) for j in range(high)]
             for j in range(high):
                 a = r + low * j
-                value = line[j].astype(BF16)
-                if width % lanes == 0:
+                value = line[j]
+                if paired:
+                    d = a * lanes // width
+                    contrib[parity if d % 2 == 0 else 1 - parity, d // 2, sl, pl.ds(a * lanes % width, lanes)] = value
+                elif width % lanes == 0:
                     contrib[a * lanes // width, sl, pl.ds(a * lanes % width, lanes)] = value
                 else:
                     for h in range(2):
                         col = a * lanes + h * cyc
                         contrib[col // width, sl, pl.ds(col % width, cyc)] = value[:, h * cyc:(h + 1) * cyc]
+        if paired:
+            @pl.when(i > 0)
+            def _():
+                twin_copy(i - 1).start()
         for c in range(chunks):
-            mine = events[len(events) * c // chunks:len(events) * (c + 1) // chunks]
-
-            @pl.when(i == c)
-            def _():
-                for q, j in mine:
-                    event(q, j)
+            if ("prep", c) in plan:
+                @pl.when(i == c)
+                def _():
+                    serve("prep", c)
         return carry
 
     lax.fori_loop(0, chunks, prep_chunk, 0)
@@ -335,37 +471,17 @@
         cols = pl.ds(*spans[c])
         return remote(contrib.at[dom ^ q, :, cols], got.at[q, :, cols], asend.at[q, c], arecv.at[q, c], to_dom(q))
 
-    paired = len(bits) == 2
-    parity = lax.rem(dom, 2)
-    last, first = 2 + 2 * parity, 4 - 2 * parity
-
-    def pair_copy(k, kind, c):
+    def half_copy(h, c):
         cols = pl.ds(*spans[c])
-        if k == 0:
-            to, slot = dom ^ 1, 1
-        else:
-            goal = k - 1
-            to = ((dom // 2) ^ (2 - goal)) * 2 + goal
-            slot = 3 - jnp.where(parity == goal, 1, 0)
-        chunk = to if kind == 0 else to ^ (2 + 2 * lax.rem(to, 2))
-        return remote(contrib.at[chunk, :, cols], got.at[slot + 4 * kind, :, cols], asend.at[2 * k + kind, c],
-                      arecv.at[slot + 4 * kind, c], {"dom": to, "cls": zed})
-
-    def arrived(slot, kind, c):
-        cols = pl.ds(*spans[c])
-        return remote(contrib.at[0, :, cols], got.at[slot + 4 * kind, :, cols], asend.at[0, c],
-                      arecv.at[slot + 4 * kind, c], to_dom(1))
+        return remote(bsend.at[h, :, :, cols], brecv.at[h, :, :, cols], asend.at[h, c], arecv.at[h, c],
+                      {"dom": dom ^ first, "cls": zed})
 
     def joined(c):
         cols = pl.ds(*spans[c])
         return remote(mid.at[:, :, cols], mgot.at[:, :, cols], jsend.at[c], jrecv.at[c], {"dom": dom ^ last, "cls": zed})
 
     if paired:
-        for kind, c in [(1, c) for c in range(len(spans))] + [(0, c) for c in range(len(spans))]:
-            for k in range(3):
-                pair_copy(k, kind, c).start()
-        got[0] = contrib[dom]
-        got[4] = contrib[dom ^ last]
+        twin_copy(chunks - 1).start()
     else:
         for c in range(len(spans)):
             for q in range(1, D):
@@ -377,6 +493,24 @@
     ids = lax.broadcasted_iota(jnp.int32, (Z * pad, rows), 0)
     gids = lax.broadcasted_iota(jnp.int32, (groups, rows), 0)
     sel_ref[...] = jnp.concatenate([jnp.where(ids == metas[d, pl.ds(0, 1), :], 1.0, 0.0).astype(BF16) for d in range(D)], axis=1)
+    if paired:
+        for i in range(chunks):
+            twin_copy(i).wait_recv()
+        for h, chip in enumerate((dom ^ first ^ last, dom ^ first, dom ^ last, dom)):
+            for c, (start, size) in enumerate(spans):
+                cols = pl.ds(start, size)
+                sums = jnp.dot(sel_ref[:, pl.ds(0, 2 * rows)], contrib[0, chip // 2, :, cols], preferred_element_type=F32)
+                sums = sums.reshape(Z, pad, size)[:, :local, :]
+                if h == 1 and c == 0:
+                    serve("sent", 0)
+                if h < 2:
+                    bsend[h, :, :, cols] = sums.astype(BF16)
+                    half_copy(h, c).start()
+                elif h == 2:
+                    keep[:, pl.ds(0, local), cols] = sums
+                else:
+                    part[:, pl.ds(0, local), cols] = sums
+        serve("summed", 0)
     gsel = jnp.concatenate([jnp.where(gids == metas[d, pl.ds(1, 1), :], 1.0, 0.0).astype(BF16) for d in range(D)], axis=1)
     counts = lax.dot_general(sel_ref[...], gsel, (((1,), (1,)), ((), ())), preferred_element_type=F32)
     wsum = jnp.dot(counts, table * table, precision=lax.Precision.HIGHEST, preferred_element_type=F32)
@@ -396,12 +530,10 @@
         start, size = spans[c]
         cols = pl.ds(start, size)
         if paired:
-            for slot in (1, 2, 3):
-                arrived(slot, 0, c).wait_recv()
-            sums = jnp.dot(sel_ref[:, pl.ds(0, 4 * rows)], got[0:4, :, cols].reshape(4 * rows, size), preferred_element_type=F32)
-            sums = sums.reshape(Z, pad, size)
+            half_copy(1, c).wait_recv()
             joined(c).wait_recv()
-            part[:, pl.ds(0, local), cols] = sums[:, :local, :] + mgot[:, :, cols].astype(F32)
+            both = brecv[1, :, :, cols].astype(F32) + mgot[:, :, cols].astype(F32)
+            part[:, pl.ds(0, local), cols] = part[:, pl.ds(0, local), cols] + both
         else:
             for q in range(1, D):
                 contrib_copy(q, c).wait()
@@ -411,10 +543,8 @@
         for j in range(1, Z):
             s_copy(j, c).start()
 
+    serve("counted", 0)
     own.wait()
-    for j in range(Z):
-        for q in offsets:
-            core_copy(q, j).wait_recv()
 
     def ref_rows(z, start, count):
         sl = pl.ds(start, count)
@@ -430,8 +560,26 @@
     whole = local // ROWS
     rest = local % ROWS
 
+    def pass_on():
+        for c, (start, size) in enumerate(spans):
+            cols = pl.ds(start, size)
+            half_copy(0, c).wait_recv()
+            mid[:, :, cols] = (keep[:, pl.ds(0, local), cols] + brecv[0, :, :, cols].astype(F32)).astype(BF16)
+            joined(c).start()
+
     def ref_step(n, carry):
-        ref_rows(n // whole, pl.multiple_of((n % whole) * ROWS, ROWS), ROWS)
+        k = n // whole
+        for c in range(Z):
+            @pl.when(n == c * whole)
+            def _():
+                if paired and c == Z - 1:
+                    pass_on()
+                serve("fft", c)
+                for q in offsets:
+                    core_copy(q, origin[c], 1).wait_recv()
+
+        z = sum(jnp.where(k == c, origin[c], 0) for c in range(Z))
+        ref_rows(z, pl.multiple_of((n % whole) * ROWS, ROWS), ROWS)
         return carry
 
     lax.fori_loop(0, Z * whole, ref_step, 0)
@@ -441,18 +589,6 @@
             return carry
         lax.fori_loop(0, Z, ref_rest, 0)
 
-    if paired:
-        near = [metas[0, pl.ds(0, 1), :], metas[1, pl.ds(0, 1), :], metas[first, pl.ds(0, 1), :], metas[first ^ 1, pl.ds(0, 1), :]]
-        sel4 = jnp.concatenate([jnp.where(ids == row, 1.0, 0.0).astype(BF16) for row in near], axis=1)
-        sel_ref[:, pl.ds(0, 4 * rows)] = sel4
-        for c, (start, size) in enumerate(spans):
-            cols = pl.ds(start, size)
-            for slot in (1, 2, 3):
-                arrived(slot, 1, c).wait_recv()
-            sums = jnp.dot(sel4, got[4:8, :, cols].reshape(4 * rows, size), preferred_element_type=F32)
-            mid[:, :, cols] = sums.reshape(Z, pad, size)[:, :local, :].astype(BF16)
-            joined(c).start()
-
     freqs = angles // 2 + 1
 
     def cross_step(m, carry):
@@ -460,10 +596,13 @@
         cross[m] = lax.dot_general(lhs, spec_p[m], (((1,), (1,)), ((), ())), preferred_element_type=F32)
         return carry
 
-    lax.fori_loop(0, freqs, cross_step, 0)
-    if paired:
-        for c in range(len(spans[:2])):
-            send_span(c)
+    group = 4
+
+    def cross_group(n, carry):
+        for g in range(group):
+            cross_step(n * group + g, carry)
+        return carry
+
     groups_of = -(-local // 8)
 
     def back_step(n, best):
@@ -477,11 +616,21 @@
         row = lax.broadcasted_iota(jnp.int32, (8, rows), 0) + j * 8
         return jnp.maximum(best, jnp.where(row < local, top, -jnp.inf))
 
-    best = lax.fori_loop(0, Z * groups_of, back_step, jnp.full((8, rows), -jnp.inf, F32))
+    pieces = freqs // group
+    half_way, in_all = (pieces + 1) // 2, Z * groups_of
+    lax.fori_loop(0, half_way, cross_group, 0)
+    send_span(0)
+    lax.fori_loop(half_way, pieces, cross_group, 0)
+    for m in range(pieces * group, freqs):
+        cross_step(m, 0)
+    for c in range(1, len(spans) - 1):
+        send_span(c)
+    best = lax.fori_loop(0, in_all // 2, back_step, jnp.full((8, rows), -jnp.inf, F32))
+    for c in range(max(1, len(spans) - 1), len(spans)):
+        send_span(c)
+    best = lax.fori_loop(in_all // 2, in_all, back_step, best)
     best_ref[...] = jnp.max(best, axis=0, keepdims=True) * (1.0 / angles)
 
-    for c in range(len(spans[:2]) if paired else 0, len(spans)):
-        send_span(c)
     weight = wpart[zed][:local, :]
     for j in range(1, Z):
         w_copy(j).wait()
@@ -498,16 +647,26 @@
     if paired:
         for c in range(len(spans)):
             joined(c).wait_send()
-            for k in range(3):
-                for kind in range(2):
-                    pair_copy(k, kind, c).wait_send()
-    for j in range(1, Z):
-        z_copy(j).wait_send()
-    for j in range(Z):
+            for h in range(2):
+                half_copy(h, c).wait_send()
+        for i in range(chunks):
+            twin_copy(i).wait_send()
+    for q in along:
+        for o in range(Z):
+            @pl.when(jnp.logical_and(o <= zed, zed + 1 < Z))
+            def _():
+                z_copy(refs_ref, q, o, True).wait_send()
+
+            @pl.when(jnp.logical_and(o >= zed, zed > 0))
+            def _():
+                z_copy(refs_ref, q, o, False).wait_send()
+    for o in range(Z):
         for q in offsets:
-            core_copy(q, j).wait_send()
-            if q:
-                plane_copy(q, last_bit(q, j), j).wait_send()
+            core_copy(q, o, 1).wait_send()
+            if q and q not in along:
+                plane_copy(q, last_bit(q, 1), o, 1).wait_send()
+    if paired:
+        plane_copy(D - 2, 2, zed, 0).wait_send()
 
 
 def per_device(particles, references, owner, class_offset, rotation, shifts, ctf_group, ctf_table):
@@ -521,6 +680,7 @@
     freqs = angles // 2 + 1
     chunks = 3
     dma = pltpu.SemaphoreType.DMA
+    paired = D == 8
     best, new = pl.pallas_call(
         lambda *refs: fused((D, Z, angles, cyc), *refs),
         out_shape=(jax.ShapeDtypeStruct((1, rows), F32), jax.ShapeDtypeStruct((local, width), F32)),
@@ -528,19 +688,19 @@
         out_specs=[pl.BlockSpec(memory_space=pltpu.VMEM)] * 2,
         scratch_shapes=[
             pltpu.VMEM((rows, full), BF16),
-            pltpu.VMEM((rows, lanes), F32),
-            pltpu.VMEM((rows, lanes), F32),
+            pltpu.VMEM((angles // 4 + 1, 3 * SPAN, 2 * lanes), BF16),
+            pltpu.VMEM((angles // 4 + 1, 2 * rows, 2 * lanes), F32),
             pltpu.VMEM((rows, lanes), F32),
             pltpu.VMEM((rows, lanes), jnp.int32),
             pltpu.VMEM((8, rows), jnp.int32),
             pltpu.VMEM((D, Z, local, width), BF16),
-            pltpu.VMEM((angles, ROWS, lanes), F32),
-            pltpu.VMEM((angles, ROWS, lanes), F32),
+            pltpu.VMEM((angles, ROWS, lanes), BF16),
+            pltpu.VMEM((angles, ROWS, lanes), BF16),
             pltpu.VMEM((freqs, 2 * rows, 2 * lanes), BF16),
             pltpu.VMEM((freqs, Z, pad, 2 * lanes), BF16),
             pltpu.VMEM((freqs, Z * pad, 2 * rows), F32),
-            pltpu.VMEM((D, rows, width), BF16),
-            pltpu.VMEM((D, rows, width), BF16),
+            pltpu.VMEM((2, D // 2, 2 * rows, width) if paired else (D, rows, width), BF16),
+            pltpu.VMEM((1, ROWS, lanes) if paired else (D, rows, width), BF16),
             pltpu.VMEM((D, 8, rows), jnp.int32),
             pltpu.VMEM((Z, pad, width), F32),
             pltpu.VMEM((Z, pad, cyc), F32),
@@ -548,13 +708,17 @@
             pltpu.VMEM((Z, local, width), BF16),
             pltpu.VMEM((Z, pad, cyc), F32),
             pltpu.VMEM((Z * pad, D * rows), BF16),
+            pltpu.VMEM((Z, pad, width) if paired else (1, 8, lanes), F32),
+            pltpu.VMEM((2, Z, local, width) if paired else (1, 1, ROWS, lanes), BF16),
+            pltpu.VMEM((2, Z, local, width) if paired else (1, 1, ROWS, lanes), BF16),
             pltpu.VMEM((Z, local, width), BF16),
             pltpu.VMEM((Z, local, width), BF16),
             dma((chunks,)), dma((chunks,)),
-            dma, dma, dma((Z,)), dma((Z,)),
+            dma, dma, dma((2, 2, Z)), dma((2, Z)),
             dma((D // 2, Z)), dma((D // 2, Z)), dma((D // 2, Z)), dma((D // 2, Z)),
             dma((D, chunks)), dma((D, chunks)), dma((D,)), dma((D,)),
             dma((Z, chunks)), dma((Z, chunks)), dma((Z,)), dma((Z,)),
+            dma((rows // ROWS,)), dma((rows // ROWS,)),
         ],
         compiler_params=pltpu.CompilerParams(collective_id=0, has_side_effects=True,
                                              vmem_limit_bytes=60 << 20),

time: 66.6 us -> 56.8 us (0.85)
  Pallas kernels: 62.5 us -> 53.1 us
    pallas_call x1, Pallas kernels: 62.5 us -> 53.1 us  [per_device(): pl.pallas_call(lambda *refs: fused((D, Z, angles, cyc), *refs), out_shape...]
where the time goes in v1:
time: 56.8 us; the launch traced here: 56.5 us
  Pallas kernels  53.1 us (93%)
  local copies, waits for them, and re-layouts  2.79 us (5%)
  between operations  0.64 us (1%)
    pallas_call x1, Pallas kernels, per_device(): pl.pallas_call(lambda *refs: fused((D, Z, angles, cyc), *refs), out_shape...  53.1 us
    unnamed x2, local copies, waits for them, and re-layouts  2.79 us

profile of v1, /device:TPU:0, one launch (start us, length us, event | category | flops | bytes accessed | tf_op | source)
XLA Modules:
  0.0 56.5 jit_solution(6494478237728961922)
XLA Ops:
  0.6 53.1 %class_pass.1 = (f32[1,128]{1,0:T(1,128)}, f32[50,1152]{1,0:T(8,128)}) custom-call(bf16[128,9216]{1,0:T(8,128)(2,1)} %refs_0_.1, bf16[50,1152]{1,0:T(8,128)(2,1)} %refs_1_.1, s32[2,128]{1,0:T(2,128)} %bitcast.6, s32[1,128]{1,0:T(1,128)} %bitcast.7, s32[1,128]{1,0:T(1,128)} %bitcast.8, s32[1,128]{1,0:T(1,128)} %bitcast.9, s32[1,128]{1,0:T(1,128)} %bitcast.10, ...), custom_call_target="tpu_custom_call" | custom-call | tf_op jit(solution)/shard_map/class_pass/pallas_call | solution.py:684
  53.7 1.1 %copy.12 = f32[128]{0:T(128)} copy(f32[128]{0:T(128)} %bitcast.11) | data formatting | bytes 1024
  54.9 1.7 %copy.13 = f32[50,1152]{1,0:T(8,128)} copy(f32[50,1152]{1,0:T(8,128)} %get-tuple-element.9) | data formatting | bytes 460800

commit v2 on v1

--- a/solution.py
+++ b/solution.py
@@ -214,7 +214,7 @@
     pad = part.shape[1]
     bits = [1 << i for i in range(1, D.bit_length() - 1)]
     offsets = list(range(0, D, 2))
-    paired = len(bits) == 2
+    paired = len(bits) == 2 and Z == 4
     parity = lax.rem(dom, 2)
     last, first = 2 + 2 * parity, 4 - 2 * parity
     along = [0, D - 2] if paired else [0]
@@ -319,9 +319,11 @@
     def children(q, h):
         return [(q ^ b, b) for b in bits if not q & b and last_bit(q ^ b, h) == b]
 
-    def event(q, h):
+    def event(q, h, only=None):
         def act(o, side):
-            if h and q in along:
+            if only == "plane":
+                pass
+            elif h and q in along:
                 z_copy(refs_ref, q, o, True).wait_recv()
                 if side < 0:
                     z_pass(block(q, o), q, o, zed >= 0, zed < 0)
@@ -331,6 +333,8 @@
                 plane_copy(q, last_bit(q, h), o, h).wait_recv()
                 if q in along:
                     z_pass(block(q, o), q, o, zed >= 0, zed >= 0)
+            if only == "line":
+                return
             if not paired or q == 0:
                 for child, b in children(q, h):
                     if not paired or child not in along:
@@ -348,25 +352,12 @@
         remote(meta_ref, metas.at[q], msend.at[q], mrecv.at[q], to_dom(q)).start()
     metas[0] = meta_ref[...]
 
-    plan = {}
-    for h in range(Z):
-        for q in sorted(offsets, key=lambda q: bin(q).count("1")):
-            hops = bin(q).count("1")
-            if not q and not h:
-                continue
-            if not paired:
-                spot = ("fft", h)
-            elif hops == 0:
-                spot = ("prep", 4) if h == 1 else ("prep", 7) if h == 2 else ("counted", 0) if h == 3 else ("fft", h - 1)
-            elif hops == 1:
-                spot = ("prep", 4) if h == 0 else ("summed", 0) if h == 1 else ("fft", h)
-            else:
-                spot = ("sent", 0) if h == 0 else ("fft", h)
-            plan.setdefault(spot, []).append((q, h))
-
-    def serve(*spot):
-        for q, h in plan.get(spot, []):
-            event(q, h)
+    plan = {("prep", 4): [(0, 1, "line")], ("prep", 5): [(2, 0), (4, 0), (0, 1, "plane")]} if paired else {}
+
+    def serve(*pairs):
+        for q, h, *part_of in pairs:
+            if h < Z:
+                event(q, h, *part_of)
 
     fetch.wait()
     chunks = rows // ROWS
@@ -456,7 +447,7 @@
             if ("prep", c) in plan:
                 @pl.when(i == c)
                 def _():
-                    serve("prep", c)
+                    serve(*plan["prep", c])
         return carry
 
     lax.fori_loop(0, chunks, prep_chunk, 0)
@@ -464,7 +455,7 @@
     spans = [(0, width)]
     if width % lanes == 0 and width // lanes >= 3:
         n = width // lanes
-        cuts = [0, n - n // 3 - max(1, n * 2 // 9), n - max(1, n * 2 // 9), n]
+        cuts = [0, n - n // 3 - max(1, n * 2 // 9), n - max(1, n // 6), n]
         spans = [(x * lanes, (y - x) * lanes) for x, y in zip(cuts[:-1], cuts[1:])]
 
     def contrib_copy(q, c):
@@ -493,24 +484,30 @@
     ids = lax.broadcasted_iota(jnp.int32, (Z * pad, rows), 0)
     gids = lax.broadcasted_iota(jnp.int32, (groups, rows), 0)
     sel_ref[...] = jnp.concatenate([jnp.where(ids == metas[d, pl.ds(0, 1), :], 1.0, 0.0).astype(BF16) for d in range(D)], axis=1)
+
+    def sum_span(c, which=(0, 1, 2, 3)):
+        start, size = spans[c]
+        cols = pl.ds(start, size)
+        for h, chip in enumerate((dom ^ first ^ last, dom ^ first, dom ^ last, dom)):
+            if h not in which:
+                continue
+            sums = jnp.dot(sel_ref[:, pl.ds(0, 2 * rows)], contrib[0, chip // 2, :, cols], preferred_element_type=F32)
+            sums = sums.reshape(Z, pad, size)[:, :local, :]
+            if h < 2:
+                bsend[h, :, :, cols] = sums.astype(BF16)
+                half_copy(h, c).start()
+            elif h == 2:
+                keep[:, pl.ds(0, local), cols] = sums
+            else:
+                part[:, pl.ds(0, local), cols] = sums
+
     if paired:
         for i in range(chunks):
             twin_copy(i).wait_recv()
-        for h, chip in enumerate((dom ^ first ^ last, dom ^ first, dom ^ last, dom)):
-            for c, (start, size) in enumerate(spans):
-                cols = pl.ds(start, size)
-                sums = jnp.dot(sel_ref[:, pl.ds(0, 2 * rows)], contrib[0, chip // 2, :, cols], preferred_element_type=F32)
-                sums = sums.reshape(Z, pad, size)[:, :local, :]
-                if h == 1 and c == 0:
-                    serve("sent", 0)
-                if h < 2:
-                    bsend[h, :, :, cols] = sums.astype(BF16)
-                    half_copy(h, c).start()
-                elif h == 2:
-                    keep[:, pl.ds(0, local), cols] = sums
-                else:
-                    part[:, pl.ds(0, local), cols] = sums
-        serve("summed", 0)
+        sum_span(0, (0,))
+        serve((0, 2))
+        sum_span(0, (1, 2, 3))
+        serve((6, 0))
     gsel = jnp.concatenate([jnp.where(gids == metas[d, pl.ds(1, 1), :], 1.0, 0.0).astype(BF16) for d in range(D)], axis=1)
     counts = lax.dot_general(sel_ref[...], gsel, (((1,), (1,)), ((), ())), preferred_element_type=F32)
     wsum = jnp.dot(counts, table * table, precision=lax.Precision.HIGHEST, preferred_element_type=F32)
@@ -543,67 +540,61 @@
         for j in range(1, Z):
             s_copy(j, c).start()
 
-    serve("counted", 0)
     own.wait()
 
-    def ref_rows(z, start, count):
+    def ref_rows(z, slot, start, count):
         sl = pl.ds(start, count)
         out = pl.ds(start, count)
 
         def store(m, re, im):
             second = jnp.zeros_like(re) if im is None else im
-            spec_r[m, z, out, pl.ds(0, lanes)] = re.astype(BF16)
-            spec_r[m, z, out, pl.ds(lanes, lanes)] = second.astype(BF16)
+            spec_r[m, slot, out, pl.ds(0, lanes)] = re.astype(BF16)
+            spec_r[m, slot, out, pl.ds(lanes, lanes)] = second.astype(BF16)
 
         forward_fft(lambda a: piece(lambda d: buf.at[d, z], sl, a).astype(F32), store, angles)
 
     whole = local // ROWS
     rest = local % ROWS
 
-    def pass_on():
-        for c, (start, size) in enumerate(spans):
-            cols = pl.ds(start, size)
-            half_copy(0, c).wait_recv()
-            mid[:, :, cols] = (keep[:, pl.ds(0, local), cols] + brecv[0, :, :, cols].astype(F32)).astype(BF16)
-            joined(c).start()
-
-    def ref_step(n, carry):
-        k = n // whole
-        for c in range(Z):
-            @pl.when(n == c * whole)
-            def _():
-                if paired and c == Z - 1:
-                    pass_on()
-                serve("fft", c)
-                for q in offsets:
-                    core_copy(q, origin[c], 1).wait_recv()
-
-        z = sum(jnp.where(k == c, origin[c], 0) for c in range(Z))
-        ref_rows(z, pl.multiple_of((n % whole) * ROWS, ROWS), ROWS)
-        return carry
-
-    lax.fori_loop(0, Z * whole, ref_step, 0)
-    if rest:
-        def ref_rest(z, carry):
-            ref_rows(z, whole * ROWS, rest)
+    def pass_on(c):
+        start, size = spans[c]
+        cols = pl.ds(start, size)
+        half_copy(0, c).wait_recv()
+        mid[:, :, cols] = (keep[:, pl.ds(0, local), cols] + brecv[0, :, :, cols].astype(F32)).astype(BF16)
+        joined(c).start()
+
+    def ref_block(k):
+        for q in offsets:
+            core_copy(q, origin[k], 1).wait_recv()
+
+        def ref_step(n, carry):
+            ref_rows(origin[k], k, pl.multiple_of(n * ROWS, ROWS), ROWS)
             return carry
-        lax.fori_loop(0, Z, ref_rest, 0)
+
+        lax.fori_loop(0, whole, ref_step, 0)
+        if rest:
+            ref_rows(origin[k], k, whole * ROWS, rest)
 
     freqs = angles // 2 + 1
-
-    def cross_step(m, carry):
-        lhs = spec_r[m].reshape(Z * pad, 2 * lanes)
-        cross[m] = lax.dot_general(lhs, spec_p[m], (((1,), (1,)), ((), ())), preferred_element_type=F32)
-        return carry
-
+    groups_of = -(-local // 8)
     group = 4
-
-    def cross_group(n, carry):
-        for g in range(group):
-            cross_step(n * group + g, carry)
-        return carry
-
-    groups_of = -(-local // 8)
+    pieces = freqs // group
+
+    def cross_step(m, lo, hi):
+        lhs = spec_r[m, pl.ds(lo, hi - lo)].reshape((hi - lo) * pad, 2 * lanes)
+        cross[m, pl.ds(lo * pad, (hi - lo) * pad), :] = lax.dot_general(
+            lhs, spec_p[m], (((1,), (1,)), ((), ())), preferred_element_type=F32)
+
+    def crosses(start, end, lo, hi):
+        def step(n, carry):
+            for g in range(group):
+                cross_step(n * group + g, lo, hi)
+            return carry
+
+        lax.fori_loop(start, min(end, pieces), step, 0)
+        if end > pieces:
+            for m in range(pieces * group, freqs):
+                cross_step(m, lo, hi)
 
     def back_step(n, best):
         z, j = n // groups_of, n % groups_of
@@ -616,19 +607,43 @@
         row = lax.broadcasted_iota(jnp.int32, (8, rows), 0) + j * 8
         return jnp.maximum(best, jnp.where(row < local, top, -jnp.inf))
 
-    pieces = freqs // group
-    half_way, in_all = (pieces + 1) // 2, Z * groups_of
-    lax.fori_loop(0, half_way, cross_group, 0)
-    send_span(0)
-    lax.fori_loop(half_way, pieces, cross_group, 0)
-    for m in range(pieces * group, freqs):
-        cross_step(m, 0)
-    for c in range(1, len(spans) - 1):
-        send_span(c)
-    best = lax.fori_loop(0, in_all // 2, back_step, jnp.full((8, rows), -jnp.inf, F32))
-    for c in range(max(1, len(spans) - 1), len(spans)):
-        send_span(c)
-    best = lax.fori_loop(in_all // 2, in_all, back_step, best)
+    def backs(start, end, best):
+        return lax.fori_loop(start, end, back_step, best)
+
+    best = jnp.full((8, rows), -jnp.inf, F32)
+    if paired:
+        most = (Z - 1) * groups_of
+        ref_block(0)
+        serve((2, 1), (4, 1))
+        sum_span(1)
+        serve((0, 3))
+        pass_on(0)
+        sum_span(2)
+        serve((6, 1))
+        ref_block(1)
+        serve((2, 2), (4, 2), (6, 2))
+        ref_block(2)
+        crosses(0, pieces // 2, 0, Z - 1)
+        send_span(0)
+        pass_on(1)
+        crosses(pieces // 2, pieces + 1, 0, Z - 1)
+        best = backs(0, most // 3, best)
+        serve(*[(q, 3) for q in (2, 4, 6)])
+        pass_on(2)
+        ref_block(Z - 1)
+        send_span(1)
+        best = backs(most // 3, most, best)
+        send_span(2)
+        crosses(0, pieces + 1, Z - 1, Z)
+        best = backs(most, Z * groups_of, best)
+    else:
+        for k in range(Z):
+            serve(*sorted([(q, k) for q in offsets if q or k], key=lambda e: bin(e[0]).count("1")))
+            ref_block(k)
+        crosses(0, pieces + 1, 0, Z)
+        best = backs(0, Z * groups_of, best)
+        for c in range(len(spans)):
+            send_span(c)
     best_ref[...] = jnp.max(best, axis=0, keepdims=True) * (1.0 / angles)
 
     weight = wpart[zed][:local, :]
@@ -680,10 +695,10 @@
     freqs = angles // 2 + 1
     chunks = 3
     dma = pltpu.SemaphoreType.DMA
-    paired = D == 8
+    paired = D == 8 and Z == 4
     best, new = pl.pallas_call(
         lambda *refs: fused((D, Z, angles, cyc), *refs),
-        out_shape=(jax.ShapeDtypeStruct((1, rows), F32), jax.ShapeDtypeStruct((local, width), F32)),
+        out_shape=(pltpu.VMEM((1, rows), F32), pltpu.VMEM((local, width), F32)),
         in_specs=[pl.BlockSpec(memory_space=pl.ANY)] * 2 + [pl.BlockSpec(memory_space=pltpu.VMEM)] * 6,
         out_specs=[pl.BlockSpec(memory_space=pltpu.VMEM)] * 2,
         scratch_shapes=[

time: 56.8 us -> 51.4 us (0.905)
  Pallas kernels: 53.1 us -> 49.4 us
  local copies, waits for them, and re-layouts: 2.79 us -> 1.21 us
    pallas_call x1, Pallas kernels: 53.1 us -> 49.4 us  [per_device(): pl.pallas_call(lambda *refs: fused((D, Z, angles, cyc), *refs), out_shape...]
    unnamed x2, local copies, waits for them, and re-layouts: 2.79 us -> 1.21 us
where the time goes in v2:
time: 51.4 us; the launch traced here: 51.3 us
  Pallas kernels  49.4 us (96%)
  local copies, waits for them, and re-layouts  1.21 us (2%)
  between operations  0.64 us (1%)
    pallas_call x1, Pallas kernels, per_device(): pl.pallas_call(lambda *refs: fused((D, Z, angles, cyc), *refs), out_shape...  49.4 us
    unnamed x2, local copies, waits for them, and re-layouts  1.21 us

profile of v2, /device:TPU:0, one launch (start us, length us, event | category | flops | bytes accessed | tf_op | source)
XLA Modules:
  0.0 51.3 jit_solution(2996786555390075968)
XLA Ops:
  0.6 49.4 %class_pass.1 = (f32[1,128]{1,0:T(1,128)S(1)}, f32[50,1152]{1,0:T(8,128)S(1)}) custom-call(bf16[128,9216]{1,0:T(8,128)(2,1)} %refs_0_.1, bf16[50,1152]{1,0:T(8,128)(2,1)} %refs_1_.1, s32[2,128]{1,0:T(2,128)} %bitcast.7, s32[1,128]{1,0:T(1,128)} %bitcast.8, s32[1,128]{1,0:T(1,128)} %bitcast.9, s32[1,128]{1,0:T(1,128)} %bitcast.10, s32[1,128]{1,0:T(1,128)} %bitcast.11, ...), custom_call_target="tpu_custom_call" | custom-call | tf_op jit(solution)/shard_map/class_pass/pallas_call | solution.py:699
  50.0 0.5 %copy.12 = f32[128]{0:T(128)} copy(f32[128]{0:T(128)S(1)} %bitcast.6) | data formatting | bytes 1024
  50.6 0.7 %copy.13 = f32[50,1152]{1,0:T(8,128)} copy(f32[50,1152]{1,0:T(8,128)S(1)} %get-tuple-element.7) | data formatting | bytes 460800

commit v3 on v2

--- a/solution.py
+++ b/solution.py
@@ -257,7 +257,7 @@
         return remote(source(q, o, h), block(q, o), psend.at[child // 2, o], precv.at[child // 2, o], to_dom(bit))
 
     def core_copy(q, o, h):
-        return remote(source(q, o, h), block(q, o), csend.at[q // 2, o], crecv.at[q // 2, o], to_dom(1))
+        return remote(source(q, o, h), block(q, o), csend, crecv.at[q // 2, o], to_dom(1))
 
     def last_bit(q, h):
         return (1 << (q.bit_length() - 1)) if h % 2 == 0 else (q & -q)
@@ -349,10 +349,10 @@
 
     event(0, 0)
     for q in range(1, D):
-        remote(meta_ref, metas.at[q], msend.at[q], mrecv.at[q], to_dom(q)).start()
+        remote(meta_ref, metas.at[q], msend, mrecv, to_dom(q)).start()
     metas[0] = meta_ref[...]
 
-    plan = {("prep", 4): [(0, 1, "line")], ("prep", 5): [(2, 0), (4, 0), (0, 1, "plane")]} if paired else {}
+    plan = {("prep", 6): [(0, 1, "line"), (2, 0), (4, 0), (0, 1, "plane")]} if paired else {}
 
     def serve(*pairs):
         for q, h, *part_of in pairs:
@@ -372,7 +372,7 @@
     def twin_copy(i):
         start = pl.multiple_of(i * ROWS, ROWS)
         return remote(contrib.at[1, :, pl.ds(start, ROWS), :], contrib.at[0, :, pl.ds(rows + start, ROWS), :],
-                      xsend.at[i], xrecv.at[i], to_dom(1))
+                      xsend, xrecv, to_dom(1))
 
     def prep_chunk(i, carry):
         sl = pl.ds(pl.multiple_of(i * ROWS, ROWS), ROWS)
@@ -455,7 +455,8 @@
     spans = [(0, width)]
     if width % lanes == 0 and width // lanes >= 3:
         n = width // lanes
-        cuts = [0, n - n // 3 - max(1, n * 2 // 9), n - max(1, n // 6), n]
+        last_cut, next_cut = n - max(1, n // 9), n - max(1, n // 9) - max(1, 2 * n // 9)
+        cuts = [0, (next_cut + 1) // 2, next_cut, last_cut, n]
         spans = [(x * lanes, (y - x) * lanes) for x, y in zip(cuts[:-1], cuts[1:])]
 
     def contrib_copy(q, c):
@@ -464,12 +465,12 @@
 
     def half_copy(h, c):
         cols = pl.ds(*spans[c])
-        return remote(bsend.at[h, :, :, cols], brecv.at[h, :, :, cols], asend.at[h, c], arecv.at[h, c],
+        return remote(bsend.at[h, :, :, cols], brecv.at[h, :, :, cols], asend.at[0, 0], arecv.at[h, c],
                       {"dom": dom ^ first, "cls": zed})
 
     def joined(c):
         cols = pl.ds(*spans[c])
-        return remote(mid.at[:, :, cols], mgot.at[:, :, cols], jsend.at[c], jrecv.at[c], {"dom": dom ^ last, "cls": zed})
+        return remote(mid.at[:, :, cols], mgot.at[:, :, cols], jsend, jrecv.at[c], {"dom": dom ^ last, "cls": zed})
 
     if paired:
         twin_copy(chunks - 1).start()
@@ -479,8 +480,8 @@
                 contrib_copy(q, c).start()
         got[0] = contrib[dom]
 
-    for q in range(1, D):
-        remote(meta_ref, metas.at[q], msend.at[q], mrecv.at[q], to_dom(q)).wait()
+    others = metas.at[pl.ds(1, D - 1)]
+    remote(others, others, msend, mrecv, to_dom(1)).wait()
     ids = lax.broadcasted_iota(jnp.int32, (Z * pad, rows), 0)
     gids = lax.broadcasted_iota(jnp.int32, (groups, rows), 0)
     sel_ref[...] = jnp.concatenate([jnp.where(ids == metas[d, pl.ds(0, 1), :], 1.0, 0.0).astype(BF16) for d in range(D)], axis=1)
@@ -502,26 +503,23 @@
                 part[:, pl.ds(0, local), cols] = sums
 
     if paired:
-        for i in range(chunks):
-            twin_copy(i).wait_recv()
-        sum_span(0, (0,))
-        serve((0, 2))
-        sum_span(0, (1, 2, 3))
-        serve((6, 0))
+        twin_all = remote(contrib.at[1, :, pl.ds(0, rows), :], contrib.at[0, :, pl.ds(rows, rows), :], xsend, xrecv, to_dom(1))
+        twin_all.wait_recv()
+        sum_span(0)
     gsel = jnp.concatenate([jnp.where(gids == metas[d, pl.ds(1, 1), :], 1.0, 0.0).astype(BF16) for d in range(D)], axis=1)
     counts = lax.dot_general(sel_ref[...], gsel, (((1,), (1,)), ((), ())), preferred_element_type=F32)
     wsum = jnp.dot(counts, table * table, precision=lax.Precision.HIGHEST, preferred_element_type=F32)
     wpart[...] = wsum.reshape(Z, pad, wsum.shape[1])
 
     def w_copy(j):
-        return remote(wpart.at[lax.rem(zed + j, Z)], wrecv.at[j], wsend.at[j], wrecv_sem.at[j], to_cls(j))
+        return remote(wpart.at[lax.rem(zed + j, Z)], wrecv.at[j], wsend, wrecv_sem, to_cls(j))
 
     for j in range(1, Z):
         w_copy(j).start()
 
     def s_copy(j, c):
         cols = pl.ds(*spans[c])
-        return remote(sbuf.at[lax.rem(zed + j, Z), :, cols], rbuf.at[j, :, cols], ssend.at[j, c], srecv.at[j, c], to_cls(j))
+        return remote(sbuf.at[lax.rem(zed + j, Z), :, cols], rbuf.at[j, :, cols], ssend, srecv.at[c], to_cls(j))
 
     def send_span(c):
         start, size = spans[c]
@@ -540,6 +538,8 @@
         for j in range(1, Z):
             s_copy(j, c).start()
 
+    if paired:
+        serve((0, 2), (6, 0))
     own.wait()
 
     def ref_rows(z, slot, start, count):
@@ -612,30 +612,33 @@
 
     best = jnp.full((8, rows), -jnp.inf, F32)
     if paired:
-        most = (Z - 1) * groups_of
+        mid_z, all_z = Z // 2, Z * groups_of
+        most = mid_z * groups_of
         ref_block(0)
         serve((2, 1), (4, 1))
         sum_span(1)
         serve((0, 3))
         pass_on(0)
-        sum_span(2)
+        for c in range(2, len(spans)):
+            sum_span(c)
         serve((6, 1))
         ref_block(1)
+        crosses(0, pieces + 1, 0, mid_z)
         serve((2, 2), (4, 2), (6, 2))
-        ref_block(2)
-        crosses(0, pieces // 2, 0, Z - 1)
         send_span(0)
         pass_on(1)
-        crosses(pieces // 2, pieces + 1, 0, Z - 1)
-        best = backs(0, most // 3, best)
+        ref_block(2)
+        best = backs(0, most, best)
+        pass_on(2)
         serve(*[(q, 3) for q in (2, 4, 6)])
-        pass_on(2)
+        send_span(1)
+        pass_on(3)
         ref_block(Z - 1)
-        send_span(1)
-        best = backs(most // 3, most, best)
+        crosses(0, pieces // 2, mid_z, Z)
         send_span(2)
-        crosses(0, pieces + 1, Z - 1, Z)
-        best = backs(most, Z * groups_of, best)
+        crosses(pieces // 2, pieces + 1, mid_z, Z)
+        send_span(3)
+        best = backs(most, all_z, best)
     else:
         for k in range(Z):
             serve(*sorted([(q, k) for q in offsets if q or k], key=lambda e: bin(e[0]).count("1")))
@@ -647,25 +650,25 @@
     best_ref[...] = jnp.max(best, axis=0, keepdims=True) * (1.0 / angles)
 
     weight = wpart[zed][:local, :]
+    w_all = wrecv.at[pl.ds(1, Z - 1)]
+    remote(w_all, w_all, wsend, wrecv_sem, to_cls(1)).wait()
     for j in range(1, Z):
-        w_copy(j).wait()
         weight = weight + wrecv[j][:local, :]
     scale = 1.0 / (jnp.concatenate([weight, weight], axis=1) + tau_reg)
     for c, (start, size) in enumerate(spans):
         cols = pl.ds(start, size)
         total = part[zed, :, cols][:local, :]
+        got_all = rbuf.at[pl.ds(1, Z - 1), :, cols]
+        remote(got_all, got_all, ssend, srecv.at[c], to_cls(1)).wait_recv()
         for j in range(1, Z):
-            s_copy(j, c).wait()
             total = total + rbuf[j, :, cols].astype(F32)
         new_ref[:, cols] = total * jnp.concatenate([scale] * -(-size // lanes), axis=1)[:, :size]
 
+    remote(sbuf.at[pl.ds(0, Z - 1)], sbuf.at[pl.ds(0, Z - 1)], ssend, srecv.at[0], to_cls(1)).wait_send()
     if paired:
-        for c in range(len(spans)):
-            joined(c).wait_send()
-            for h in range(2):
-                half_copy(h, c).wait_send()
-        for i in range(chunks):
-            twin_copy(i).wait_send()
+        remote(mid, mgot, jsend, jrecv.at[0], to_dom(1)).wait_send()
+        remote(bsend, brecv, asend.at[0, 0], arecv.at[0, 0], to_dom(1)).wait_send()
+        twin_all.wait_send()
     for q in along:
         for o in range(Z):
             @pl.when(jnp.logical_and(o <= zed, zed + 1 < Z))
@@ -675,9 +678,9 @@
             @pl.when(jnp.logical_and(o >= zed, zed > 0))
             def _():
                 z_copy(refs_ref, q, o, False).wait_send()
+    remote(buf.at[pl.ds(0, D // 2)], buf.at[pl.ds(0, D // 2)], csend, crecv.at[0, 0], to_dom(1)).wait_send()
     for o in range(Z):
         for q in offsets:
-            core_copy(q, o, 1).wait_send()
             if q and q not in along:
                 plane_copy(q, last_bit(q, 1), o, 1).wait_send()
     if paired:
@@ -693,7 +696,7 @@
     local, width = references.shape
     pad = -(-local // ROWS) * ROWS
     freqs = angles // 2 + 1
-    chunks = 3
+    chunks = 4
     dma = pltpu.SemaphoreType.DMA
     paired = D == 8 and Z == 4
     best, new = pl.pallas_call(
@@ -728,12 +731,11 @@
             pltpu.VMEM((2, Z, local, width) if paired else (1, 1, ROWS, lanes), BF16),
             pltpu.VMEM((Z, local, width), BF16),
             pltpu.VMEM((Z, local, width), BF16),
-            dma((chunks,)), dma((chunks,)),
+            dma, dma((chunks,)),
             dma, dma, dma((2, 2, Z)), dma((2, Z)),
-            dma((D // 2, Z)), dma((D // 2, Z)), dma((D // 2, Z)), dma((D // 2, Z)),
-            dma((D, chunks)), dma((D, chunks)), dma((D,)), dma((D,)),
-            dma((Z, chunks)), dma((Z, chunks)), dma((Z,)), dma((Z,)),
-            dma((rows // ROWS,)), dma((rows // ROWS,)),
+            dma((D // 2, Z)), dma((D // 2, Z)), dma, dma((D // 2, Z)),
+            dma((1, 1) if paired else (D, chunks)), dma((2 if paired else D, chunks)), dma, dma,
+            dma, dma((chunks,)), dma, dma, dma, dma,
         ],
         compiler_params=pltpu.CompilerParams(collective_id=0, has_side_effects=True,
                                              vmem_limit_bytes=60 << 20),

time: 51.4 us -> 48.7 us (0.947)
  Pallas kernels: 49.4 us -> 46.7 us
    pallas_call x1, Pallas kernels: 49.4 us -> 46.7 us  [per_device(): pl.pallas_call(lambda *refs: fused((D, Z, angles, cyc), *refs), out_shape...]
where the time goes in v3:
time: 48.7 us; the launch traced here: 48.5 us
  Pallas kernels  46.7 us (96%)
  local copies, waits for them, and re-layouts  1.21 us (2%)
  between operations  0.64 us (1%)
    pallas_call x1, Pallas kernels, per_device(): pl.pallas_call(lambda *refs: fused((D, Z, angles, cyc), *refs), out_shape...  46.7 us
    unnamed x2, local copies, waits for them, and re-layouts  1.21 us

profile of v3, /device:TPU:0, one launch (start us, length us, event | category | flops | bytes accessed | tf_op | source)
XLA Modules:
  0.0 48.5 jit_solution(14358329202179010984)
XLA Ops:
  0.6 46.7 %class_pass.1 = (f32[1,128]{1,0:T(1,128)S(1)}, f32[50,1152]{1,0:T(8,128)S(1)}) custom-call(bf16[128,9216]{1,0:T(8,128)(2,1)} %refs_0_.1, bf16[50,1152]{1,0:T(8,128)(2,1)} %refs_1_.1, s32[2,128]{1,0:T(2,128)} %bitcast.7, s32[1,128]{1,0:T(1,128)} %bitcast.8, s32[1,128]{1,0:T(1,128)} %bitcast.9, s32[1,128]{1,0:T(1,128)} %bitcast.10, s32[1,128]{1,0:T(1,128)} %bitcast.11, ...), custom_call_target="tpu_custom_call" | custom-call | tf_op jit(solution)/shard_map/class_pass/pallas_call | solution.py:702
  47.3 0.5 %copy.12 = f32[128]{0:T(128)} copy(f32[128]{0:T(128)S(1)} %bitcast.6) | data formatting | bytes 1024
  47.8 0.7 %copy.13 = f32[50,1152]{1,0:T(8,128)} copy(f32[50,1152]{1,0:T(8,128)S(1)} %get-tuple-element.7) | data formatting | bytes 460800

commit v4 on v3

--- a/solution.py
+++ b/solution.py
@@ -254,10 +254,10 @@
 
     def plane_copy(child, bit, o, h):
         q = child ^ bit
-        return remote(source(q, o, h), block(q, o), psend.at[child // 2, o], precv.at[child // 2, o], to_dom(bit))
+        return remote(source(q, o, h), block(q, o), psend, precv.at[child // 2, o], to_dom(bit))
 
     def core_copy(q, o, h):
-        return remote(source(q, o, h), block(q, o), csend, crecv.at[q // 2, o], to_dom(1))
+        return remote(source(q, o, h), block(q, o), csend, crecv.at[o], to_dom(1))
 
     def last_bit(q, h):
         return (1 << (q.bit_length() - 1)) if h % 2 == 0 else (q & -q)
@@ -456,7 +456,7 @@
     if width % lanes == 0 and width // lanes >= 3:
         n = width // lanes
         last_cut, next_cut = n - max(1, n // 9), n - max(1, n // 9) - max(1, 2 * n // 9)
-        cuts = [0, (next_cut + 1) // 2, next_cut, last_cut, n]
+        cuts = [0, 2 * next_cut // 3, next_cut, last_cut, n]
         spans = [(x * lanes, (y - x) * lanes) for x, y in zip(cuts[:-1], cuts[1:])]
 
     def contrib_copy(q, c):
@@ -535,8 +535,8 @@
             sums = jnp.dot(sel_ref[...], got[:, :, cols].reshape(D * rows, size), preferred_element_type=F32)
             part[:, :, cols] = sums.reshape(Z, pad, size)
         sbuf[:, :, cols] = part[:, pl.ds(0, local), cols].astype(BF16)
-        for j in range(1, Z):
-            s_copy(j, c).start()
+        for h in reversed(range(1, Z)):
+            at_hops(h, lambda o, side: s_copy(lax.rem(o - zed + Z, Z), c).start())
 
     if paired:
         serve((0, 2), (6, 0))
@@ -564,8 +564,8 @@
         joined(c).start()
 
     def ref_block(k):
-        for q in offsets:
-            core_copy(q, origin[k], 1).wait_recv()
+        came = buf.at[pl.ds(0, D // 2), origin[k]]
+        remote(came, came, csend, crecv.at[origin[k]], to_dom(1)).wait_recv()
 
         def ref_step(n, carry):
             ref_rows(origin[k], k, pl.multiple_of(n * ROWS, ROWS), ROWS)
@@ -616,11 +616,14 @@
         most = mid_z * groups_of
         ref_block(0)
         serve((2, 1), (4, 1))
-        sum_span(1)
+        sum_span(1, (0, 2, 3))
         serve((0, 3))
         pass_on(0)
         for c in range(2, len(spans)):
-            sum_span(c)
+            sum_span(c, (0,))
+        sum_span(1, (1,))
+        for c in range(2, len(spans)):
+            sum_span(c, (1, 2, 3))
         serve((6, 1))
         ref_block(1)
         crosses(0, pieces + 1, 0, mid_z)
@@ -628,16 +631,18 @@
         send_span(0)
         pass_on(1)
         ref_block(2)
-        best = backs(0, most, best)
+        best = backs(0, most // 2, best)
         pass_on(2)
+        best = backs(most // 2, most, best)
+        pass_on(3)
         serve(*[(q, 3) for q in (2, 4, 6)])
         send_span(1)
-        pass_on(3)
         ref_block(Z - 1)
         crosses(0, pieces // 2, mid_z, Z)
         send_span(2)
-        crosses(pieces // 2, pieces + 1, mid_z, Z)
+        crosses(pieces // 2, 3 * pieces // 4, mid_z, Z)
         send_span(3)
+        crosses(3 * pieces // 4, pieces + 1, mid_z, Z)
         best = backs(most, all_z, best)
     else:
         for k in range(Z):
@@ -678,13 +683,9 @@
             @pl.when(jnp.logical_and(o >= zed, zed > 0))
             def _():
                 z_copy(refs_ref, q, o, False).wait_send()
-    remote(buf.at[pl.ds(0, D // 2)], buf.at[pl.ds(0, D // 2)], csend, crecv.at[0, 0], to_dom(1)).wait_send()
-    for o in range(Z):
-        for q in offsets:
-            if q and q not in along:
-                plane_copy(q, last_bit(q, 1), o, 1).wait_send()
-    if paired:
-        plane_copy(D - 2, 2, zed, 0).wait_send()
+    remote(buf.at[pl.ds(0, D // 2)], buf.at[pl.ds(0, D // 2)], csend, crecv.at[0], to_dom(1)).wait_send()
+    sent = buf.at[pl.ds(0, 3), pl.ds(0, 3)] if paired else buf.at[pl.ds(0, D // 2 - 1)]
+    remote(sent, sent, psend, precv.at[0, 0], to_dom(2)).wait_send()
 
 
 def per_device(particles, references, owner, class_offset, rotation, shifts, ctf_group, ctf_table):
@@ -733,7 +734,7 @@
             pltpu.VMEM((Z, local, width), BF16),
             dma, dma((chunks,)),
             dma, dma, dma((2, 2, Z)), dma((2, Z)),
-            dma((D // 2, Z)), dma((D // 2, Z)), dma, dma((D // 2, Z)),
+            dma, dma((D // 2, Z)), dma, dma((Z,)),
             dma((1, 1) if paired else (D, chunks)), dma((2 if paired else D, chunks)), dma, dma,
             dma, dma((chunks,)), dma, dma, dma, dma,
         ],

time: 48.7 us -> 48.2 us (0.990)
  Pallas kernels: 46.7 us -> 46.1 us
    pallas_call x1, Pallas kernels: 46.7 us -> 46.1 us  [per_device(): pl.pallas_call(lambda *refs: fused((D, Z, angles, cyc), *refs), out_shape...]
where the time goes in v4:
time: 48.2 us; the launch traced here: 48 us
  Pallas kernels  46.1 us (96%)
  local copies, waits for them, and re-layouts  1.21 us (3%)
  between operations  0.64 us (1%)
    pallas_call x1, Pallas kernels, per_device(): pl.pallas_call(lambda *refs: fused((D, Z, angles, cyc), *refs), out_shape...  46.1 us
    unnamed x2, local copies, waits for them, and re-layouts  1.21 us

profile of v4, /device:TPU:0, one launch (start us, length us, event | category | flops | bytes accessed | tf_op | source)
XLA Modules:
  0.0 48.0 jit_solution(1200379741507484788)
XLA Ops:
  0.6 46.1 %class_pass.1 = (f32[1,128]{1,0:T(1,128)S(1)}, f32[50,1152]{1,0:T(8,128)S(1)}) custom-call(bf16[128,9216]{1,0:T(8,128)(2,1)} %refs_0_.1, bf16[50,1152]{1,0:T(8,128)(2,1)} %refs_1_.1, s32[2,128]{1,0:T(2,128)} %bitcast.7, s32[1,128]{1,0:T(1,128)} %bitcast.8, s32[1,128]{1,0:T(1,128)} %bitcast.9, s32[1,128]{1,0:T(1,128)} %bitcast.10, s32[1,128]{1,0:T(1,128)} %bitcast.11, ...), custom_call_target="tpu_custom_call" | custom-call | tf_op jit(solution)/shard_map/class_pass/pallas_call | solution.py:703
  46.8 0.5 %copy.12 = f32[128]{0:T(128)} copy(f32[128]{0:T(128)S(1)} %bitcast.6) | data formatting | bytes 1024
  47.3 0.7 %copy.13 = f32[50,1152]{1,0:T(8,128)} copy(f32[50,1152]{1,0:T(8,128)S(1)} %get-tuple-element.7) | data formatting | bytes 460800

commit v5 on v4

--- a/solution.py
+++ b/solution.py
@@ -618,25 +618,36 @@
         serve((2, 1), (4, 1))
         sum_span(1, (0, 2, 3))
         serve((0, 3))
+        inner = jnp.logical_and(zed > 0, zed + 1 < Z)
+
+        def serve_when(cond, *pairs):
+            @pl.when(cond)
+            def _():
+                serve(*pairs)
+
+        serve_when(inner, (6, 1))
         pass_on(0)
         for c in range(2, len(spans)):
             sum_span(c, (0,))
         sum_span(1, (1,))
         for c in range(2, len(spans)):
             sum_span(c, (1, 2, 3))
-        serve((6, 1))
+        serve_when(jnp.logical_not(inner), (6, 1))
         ref_block(1)
-        crosses(0, pieces + 1, 0, mid_z)
-        serve((2, 2), (4, 2), (6, 2))
-        send_span(0)
+        crosses(0, pieces // 2, 0, mid_z)
+        serve_when(inner, (6, 2))
+        crosses(pieces // 2, pieces + 1, 0, mid_z)
+        serve((2, 2), (4, 2))
+        serve_when(jnp.logical_not(inner), (6, 2))
         pass_on(1)
         ref_block(2)
+        send_span(0)
         best = backs(0, most // 2, best)
         pass_on(2)
         best = backs(most // 2, most, best)
         pass_on(3)
+        send_span(1)
         serve(*[(q, 3) for q in (2, 4, 6)])
-        send_span(1)
         ref_block(Z - 1)
         crosses(0, pieces // 2, mid_z, Z)
         send_span(2)

time: 48.2 us -> 47.9 us (level)
  no operation moved by 1% of the time
where the time goes in v5:
time: 47.9 us; the launch traced here: 47.7 us
  Pallas kernels  45.8 us (96%)
  local copies, waits for them, and re-layouts  1.21 us (3%)
  between operations  0.64 us (1%)
    pallas_call x1, Pallas kernels, per_device(): pl.pallas_call(lambda *refs: fused((D, Z, angles, cyc), *refs), out_shape...  45.8 us
    unnamed x2, local copies, waits for them, and re-layouts  1.21 us

profile of v5, /device:TPU:0, one launch (start us, length us, event | category | flops | bytes accessed | tf_op | source)
XLA Modules:
  0.0 47.7 jit_solution(11081897285832320001)
XLA Ops:
  0.6 45.8 %class_pass.1 = (f32[1,128]{1,0:T(1,128)S(1)}, f32[50,1152]{1,0:T(8,128)S(1)}) custom-call(bf16[128,9216]{1,0:T(8,128)(2,1)} %refs_0_.1, bf16[50,1152]{1,0:T(8,128)(2,1)} %refs_1_.1, s32[2,128]{1,0:T(2,128)} %bitcast.7, s32[1,128]{1,0:T(1,128)} %bitcast.8, s32[1,128]{1,0:T(1,128)} %bitcast.9, s32[1,128]{1,0:T(1,128)} %bitcast.10, s32[1,128]{1,0:T(1,128)} %bitcast.11, ...), custom_call_target="tpu_custom_call" | custom-call | tf_op jit(solution)/shard_map/class_pass/pallas_call | solution.py:714
  46.5 0.5 %copy.12 = f32[128]{0:T(128)} copy(f32[128]{0:T(128)S(1)} %bitcast.6) | data formatting | bytes 1024
  47.0 0.7 %copy.13 = f32[50,1152]{1,0:T(8,128)} copy(f32[50,1152]{1,0:T(8,128)S(1)} %get-tuple-element.7) | data formatting | bytes 460800
